TPU v7x, 256 devices: a whole 4x4x8 slice. The times are simulated.
256 devices in a mesh: tm: 4 (over x_hi, core), space: 64 (over x_lo, y, z).
Axes of the slice: x: 4 (x_hi: 2, x_lo: 2; x = x_hi * 2 + x_lo), y: 4, z: 8, core: 2. Of those that a mesh axis runs over, the one named last changes fastest.
Arguments:
- latent_tokens: bfloat16 [16, 64, 64, 64], P('tm', None, 'space'), may hold values from -12 to 12
- conv_in_weight: bfloat16 [3, 3, 3, 16, 384], replicated, may hold values from -0.3125 to 0.3125
- conv_in_bias: float32 [384], replicated, may hold values from -3 to 3
- norm_gain: float32 [384], replicated, may hold values from 0.25 to 1.75
- conv_mid_weight: bfloat16 [3, 3, 3, 384, 384], replicated, may hold values from -0.0625 to 0.0625
- conv_mid_bias: float32 [384], replicated, may hold values from -3 to 3
Outputs:
- decoded: bfloat16 [16, 128, 128, 384], P('tm', 'space')
All inputs are finite; a program needn't handle non-finite values.
Results may differ from a plain program's by a relative error of at most 0.005.
Values may be sent and summed in bfloat16 or wider, within the bound.
A program may use at most 128 MiB of HBM per device.

v0:
```python
import jax
import jax.numpy as jnp
from jax import lax
from jax.sharding import PartitionSpec as P


def padded_2(cells, sides, width):
    for axis, dim in sides:
        count = lax.axis_size(axis)
        ends = count - 1
        head = lax.slice_in_dim(cells, 0, width, axis=dim)
        tail = lax.slice_in_dim(cells, cells.shape[dim] - width, cells.shape[dim], axis=dim)
        cells = jnp.concatenate(
            [
                lax.ppermute(tail, axis, [(i, (i + 1) % count) for i in range(ends)]),
                cells,
                lax.ppermute(head, axis, [((i + 1) % count, i) for i in range(ends)]),
            ],
            axis=dim,
        )
    return cells


def shifted(value, axis, steps):
    count = lax.axis_size(axis)
    initial, last = (max(0, -steps), min(count, count - steps))
    return lax.ppermute(value, axis, [(source, source + steps) for source in range(initial, last)])


def causal_conv(padded, weight):
    frames = padded.shape[0] - 2
    height = padded.shape[1] - 2
    breadth = padded.shape[2] - 2
    summed = jnp.zeros((frames * height * breadth, weight.shape[-1]), jnp.float32)
    for tap_time in range(3):
        for tap_row in range(3):
            for tap_col in range(3):
                window = padded[
                    tap_time : tap_time + frames,
                    tap_row : tap_row + height,
                    tap_col : tap_col + breadth,
                ]
                summed = summed + jnp.dot(
                    window.reshape(-1, window.shape[-1]),
                    weight[tap_time, tap_row, tap_col],
                    preferred_element_type=jnp.float32,
                )
    return summed.reshape(frames, height, breadth, weight.shape[-1])


def unfold_conv(padded, weight):
    frames = padded.shape[0] - 2
    height = padded.shape[1] - 2
    breadth = padded.shape[2] - 2
    windows = []
    for tap_time in range(3):
        for tap_row in range(3):
            for tap_col in range(3):
                windows.append(
                    padded[
                        tap_time : tap_time + frames,
                        tap_row : tap_row + height,
                        tap_col : tap_col + breadth,
                    ]
                )
    stacked = jnp.concatenate(windows, axis=-1)
    flat_weight = weight.reshape(-1, weight.shape[-1])
    summed = jnp.dot(
        stacked.reshape(-1, stacked.shape[-1]), flat_weight, preferred_element_type=jnp.float32
    )
    return summed.reshape(frames, height, breadth, weight.shape[-1])


def unpatch(tokens):
    frames, height, breadth, _ = tokens.shape
    grid = tokens.reshape(frames, height, breadth, 2, 2, -1).transpose(0, 1, 3, 2, 4, 5)
    return grid.reshape(frames, 2 * height, 2 * breadth, -1)


def activate(feature, norm_gain):
    values = feature.astype(jnp.float32)
    spread = jnp.sqrt(jnp.mean(values * values, axis=-1, keepdims=True) + 1e-06)
    return jax.nn.silu(values / spread * norm_gain).astype(jnp.bfloat16)


def pad_columns(source):
    return jnp.pad(source, ((0, 0), (0, 0), (1, 1), (0, 0)))


def per_device(
    latent_tokens, conv_in_weight, conv_in_bias, norm_gain, conv_mid_weight, conv_mid_bias
):
    tiled = lax.all_to_all(latent_tokens, "space", split_axis=1, concat_axis=2, tiled=True)
    latents = unpatch(tiled)
    frames_here = latents.shape[0]
    rows_ext = padded_2(latents, (("space", 1),), 1)
    cache_rows = shifted(rows_ext[frames_here - 2 :], "tm", 1)
    padded = pad_columns(jnp.concatenate([cache_rows, rows_ext], 0))
    feature = (unfold_conv(padded, conv_in_weight) + conv_in_bias).astype(jnp.bfloat16)
    activated = activate(feature, norm_gain)
    act_ext = padded_2(activated, (("space", 1),), 1)
    act_cache = shifted(act_ext[frames_here - 2 :], "tm", 1)
    padded_act = pad_columns(jnp.concatenate([act_cache, act_ext], 0))
    mixed_sum = causal_conv(padded_act, conv_mid_weight)
    decoded = (feature.astype(jnp.float32) + mixed_sum + conv_mid_bias).astype(jnp.bfloat16)
    return decoded


def solution(mesh):
    return jax.shard_map(
        per_device,
        mesh=mesh,
        in_specs=(P("tm", None, "space", None), P(), P(), P(), P(), P()),
        out_specs=P("tm", "space", None, None),
        check_vma=False,
    )
```

profile of v0, /device:TPU:6, one launch (start us, length us, event | category | flops | bytes accessed | tf_op | source)
XLA Modules:
  0.0 144.5 jit_solution(10468853418308770894)
XLA Ops:
  1.0 22.7 %all_to_all.4 = bf16[64,2,128]{2,1,0:T(2,128)(2,1)S(1)} all-to-all(bf16[64,2,128]{2,1,0:T(2,128)(2,1)S(1)} %reshape.144), channel_id=1, replica_groups=mesh['tm'=4,'space'=64] {'space'}, dimensions={0} | all-to-all | bytes 65536 | tf_op jit(solution)/shard_map/all_to_all | solution.py:93
  24.2 2.5 %collective-permute-start = (bf16[4,1,128,16]{2,3,1,0:T(8,128)(2,1)S(1)}, bf16[4,1,128,16]{2,3,1,0:T(8,128)(2,1)S(1)}, u32[]{:S(2)}, u32[]{:S(2)}) collective-permute-start(bf16[4,1,128,16]{2,3,1,0:T(8,128)(2,1)S(1)} %get-tuple-element.33), channel_id=1, source_target_pairs={{0,1},{1,2},{2,3},{3,4},{4,5},{5,6},{6,7},{7,8},{8,9},{9,10},{10,1... | collective-permute-start | bytes 49160 | tf_op jit(solution)/shard_map/ppermute | solution.py:15
  26.7 7.6 %collective-permute-start.1 = (bf16[4,1,128,16]{2,3,1,0:T(8,128)(2,1)S(1)}, bf16[4,1,128,16]{2,3,1,0:T(8,128)(2,1)S(1)}, u32[]{:S(2)}, u32[]{:S(2)}) collective-permute-start(bf16[4,1,128,16]{2,3,1,0:T(8,128)(2,1)S(1)} %get-tuple-element.34), channel_id=1, source_target_pairs={{1,0},{2,1},{3,2},{4,3},{5,4},{6,5},{7,6},{8,7},{9,8},{10,9},{11,1... | collective-permute-start | bytes 49160 | tf_op jit(solution)/shard_map/ppermute | solution.py:17
  35.7 1.9 %collective-permute-start.2 = (bf16[2,4,128,16]{2,3,1,0:T(8,128)(2,1)S(1)}, bf16[2,4,128,16]{2,3,1,0:T(8,128)(2,1)S(1)}, u32[]{:S(2)}, u32[]{:S(2)}) collective-permute-start(bf16[2,4,128,16]{2,3,1,0:T(8,128)(2,1)S(1)} %pad_maximum_fusion.6), channel_id=1, source_target_pairs={{0,64},{64,128},{128,192},{1,65},{65,129},{129,193},{2,66},{66,130... | collective-permute-start | bytes 98312 | tf_op jit(solution)/shard_map/ppermute | solution.py:27
  37.7 4.8 %collective-permute-done.2 = bf16[2,4,128,16]{2,3,1,0:T(8,128)(2,1)S(1)} collective-permute-done((bf16[2,4,128,16]{2,3,1,0:T(8,128)(2,1)S(1)}, bf16[2,4,128,16]{2,3,1,0:T(8,128)(2,1)S(1)}, u32[]{:S(2)}, u32[]{:S(2)}) %collective-permute-start.2) | collective-permute-done | bytes 32800 | tf_op jit(solution)/shard_map/ppermute | solution.py:27
  46.0 2.2 %collective-permute-start.3 = (bf16[4,1,128,384]{3,2,1,0:T(8,128)(2,1)S(1)}, bf16[4,1,128,384]{3,2,1,0:T(8,128)(2,1)S(1)}, u32[]{:S(2)}, u32[]{:S(2)}) collective-permute-start(bf16[4,1,128,384]{3,2,1,0:T(8,128)(2,1)S(1)} %get-tuple-element.31), channel_id=1, source_target_pairs={{0,1},{1,2},{2,3},{3,4},{4,5},{5,6},{6,7},{7,8},{8,9},{9,10},{10,1... | collective-permute-start | bytes 1179656 | tf_op jit(solution)/shard_map/ppermute | solution.py:15
  48.2 8.4 %collective-permute-start.4 = (bf16[4,1,128,384]{3,2,1,0:T(8,128)(2,1)S(1)}, bf16[4,1,128,384]{3,2,1,0:T(8,128)(2,1)S(1)}, u32[]{:S(2)}, u32[]{:S(2)}) collective-permute-start(bf16[4,1,128,384]{3,2,1,0:T(8,128)(2,1)S(1)} %get-tuple-element.32), channel_id=1, source_target_pairs={{1,0},{2,1},{3,2},{4,3},{5,4},{6,5},{7,6},{8,7},{9,8},{10,9},{11,1... | collective-permute-start | bytes 1179656 | tf_op jit(solution)/shard_map/ppermute | solution.py:17
  56.7 3.8 %collective-permute-done.3 = bf16[4,1,128,384]{3,2,1,0:T(8,128)(2,1)S(1)} collective-permute-done((bf16[4,1,128,384]{3,2,1,0:T(8,128)(2,1)S(1)}, bf16[4,1,128,384]{3,2,1,0:T(8,128)(2,1)S(1)}, u32[]{:S(2)}, u32[]{:S(2)}) %collective-permute-start.3) | collective-permute-done | bytes 393248 | tf_op jit(solution)/shard_map/ppermute | solution.py:15
  62.0 1.9 %collective-permute-start.5 = (bf16[2,4,128,384]{3,2,1,0:T(8,128)(2,1)S(1)}, bf16[2,4,128,384]{3,2,1,0:T(8,128)(2,1)S(1)}, u32[]{:S(2)}, u32[]{:S(2)}) collective-permute-start(bf16[2,4,128,384]{3,2,1,0:T(8,128)(2,1)S(1)} %pad_maximum_fusion.2), channel_id=1, source_target_pairs={{0,64},{64,128},{128,192},{1,65},{65,129},{129,193},{2,66},{66,130... | collective-permute-start | bytes 2359304 | tf_op jit(solution)/shard_map/ppermute | solution.py:27
  66.1 10.8 %collective-permute-done.5 = bf16[2,4,128,384]{3,2,1,0:T(8,128)(2,1)S(1)} collective-permute-done((bf16[2,4,128,384]{3,2,1,0:T(8,128)(2,1)S(1)}, bf16[2,4,128,384]{3,2,1,0:T(8,128)(2,1)S(1)}, u32[]{:S(2)}, u32[]{:S(2)}) %collective-permute-start.5) | collective-permute-done | bytes 786464 | tf_op jit(solution)/shard_map/ppermute | solution.py:27
  77.6 4.4 %pad_slice_fusion.18 = (bf16[4,2,128,384]{3,2,1,0:T(8,128)(2,1)}, bf16[4,2,128,384]{3,2,1,0:T(8,128)(2,1)S(1)}, bf16[4,2,128,384]{3,2,1,0:T(8,128)(2,1)S(1)}, bf...) fusion(bf16[6,4,128,384]{3,2,1,0:T(8,128)(2,1)S(1)} %maximum_ma, ...), kind=kLoop, calls=%fused_computation.147 | loop fusion | bytes 11010048 | tf_op jit(solution)/shard_map/slice | solution.py:38
  82.0 3.4 %fusion.87 = (bf16[4,2,128,384]{3,2,1,0:T(8,128)(2,1)S(1)}, bf16[4,2,128,384]{3,2,1,0:T(8,128)(2,1)S(1)}, bf16[4,2,128,384]{3,2,1,0:T(8,128)(2,1)S(1)}, bf16[4,2...) fusion(bf16[6,4,128,384]{3,2,1,0:T(8,128)(2,1)S(1)} %maximum_ma, ...), kind=kLoop, calls=%fused_computation.165 | loop fusion | bytes 13369344 | tf_op jit(solution)/shard_map/slice | solution.py:38
  87.2 1.9 %fusion.58 = f32[1024,384]{1,0:T(8,128)} fusion(bf16[1024,384]{1,0:T(8,128)(2,1)S(1)} %bitcast.168, bf16[3,3,3,384,384]{4,3,2,1,0:T(8,128)(2,1)S(1)} %copy-done.2), kind=kOutput, calls=%fused_computation.85 | convolution fusion | flops 301989888 | bytes 2654208 | tf_op jit(solution)/shard_map/dot_general | solution.py:43
  89.0 1.8 %fusion.50 = f32[1024,384]{1,0:T(8,128)} fusion(bf16[1024,384]{1,0:T(8,128)(2,1)S(1)} %bitcast.167, bf16[3,3,3,384,384]{4,3,2,1,0:T(8,128)(2,1)S(1)} %copy-done.2), kind=kOutput, calls=%fused_computation.77 | convolution fusion | flops 301989888 | bytes 2654208 | tf_op jit(solution)/shard_map/dot_general | solution.py:43
  92.7 1.8 %fusion.52 = f32[1024,384]{1,0:T(8,128)} fusion(bf16[1024,384]{1,0:T(8,128)(2,1)S(1)} %bitcast.179, bf16[3,3,3,384,384]{4,3,2,1,0:T(8,128)(2,1)S(1)} %copy-done.2), kind=kOutput, calls=%fused_computation.79 | convolution fusion | flops 301989888 | bytes 2654208 | tf_op jit(solution)/shard_map/dot_general | solution.py:43
  98.1 1.8 %fusion.42 = f32[1024,384]{1,0:T(8,128)} fusion(bf16[1024,384]{1,0:T(8,128)(2,1)S(1)} %bitcast.176, bf16[3,3,3,384,384]{4,3,2,1,0:T(8,128)(2,1)S(1)} %copy-done.2), kind=kOutput, calls=%fused_computation.69 | convolution fusion | flops 301989888 | bytes 2654208 | tf_op jit(solution)/shard_map/dot_general | solution.py:43
  103.4 1.8 %fusion.34 = f32[1024,384]{1,0:T(8,128)} fusion(bf16[1024,384]{1,0:T(8,128)(2,1)S(1)} %bitcast.173, bf16[3,3,3,384,384]{4,3,2,1,0:T(8,128)(2,1)S(1)} %copy-done.2), kind=kOutput, calls=%fused_computation.61 | convolution fusion | flops 301989888 | bytes 2654208 | tf_op jit(solution)/shard_map/dot_general | solution.py:43
  105.2 1.9 %fusion.26 = f32[1024,384]{1,0:T(8,128)} fusion(bf16[1024,384]{1,0:T(8,128)(2,1)S(1)} %bitcast.172, bf16[3,3,3,384,384]{4,3,2,1,0:T(8,128)(2,1)S(1)} %copy-done.2), kind=kOutput, calls=%fused_computation.53 | convolution fusion | flops 301989888 | bytes 2654208 | tf_op jit(solution)/shard_map/dot_general | solution.py:43
  107.1 1.8 %fusion.30 = f32[1024,384]{1,0:T(8,128)} fusion(bf16[1024,384]{1,0:T(8,128)(2,1)S(1)} %bitcast.166, bf16[3,3,3,384,384]{4,3,2,1,0:T(8,128)(2,1)S(1)} %copy-done.2), kind=kOutput, calls=%fused_computation.57 | convolution fusion | flops 301989888 | bytes 2654208 | tf_op jit(solution)/shard_map/dot_general | solution.py:43
  114.2 1.8 %fusion.22 = f32[1024,384]{1,0:T(8,128)} fusion(bf16[1024,384]{1,0:T(8,128)(2,1)S(1)} %bitcast.162, bf16[3,3,3,384,384]{4,3,2,1,0:T(8,128)(2,1)S(1)} %copy-done.2), kind=kOutput, calls=%fused_computation.49 | convolution fusion | flops 301989888 | bytes 2654208 | tf_op jit(solution)/shard_map/dot_general | solution.py:43
  119.6 1.8 %fusion.12 = f32[1024,384]{1,0:T(8,128)} fusion(bf16[1024,384]{1,0:T(8,128)(2,1)S(1)} %bitcast.159, bf16[3,3,3,384,384]{4,3,2,1,0:T(8,128)(2,1)S(1)} %copy-done.2), kind=kOutput, calls=%fused_computation.39 | convolution fusion | flops 301989888 | bytes 2654208 | tf_op jit(solution)/shard_map/dot_general | solution.py:43
  121.4 2.0 %fusion.10 = f32[1024,384]{1,0:T(8,128)} fusion(bf16[1024,384]{1,0:T(8,128)(2,1)S(1)} %bitcast.158, bf16[3,3,3,384,384]{4,3,2,1,0:T(8,128)(2,1)S(1)} %copy-done.2), kind=kOutput, calls=%fused_computation.37 | convolution fusion | flops 301989888 | bytes 2654208 | tf_op jit(solution)/shard_map/dot_general | solution.py:43
  126.9 14.9 %add_add_fusion = f32[1024,384]{1,0:T(8,128)} fusion(f32[1024,384]{1,0:T(8,128)S(1)} %fusion.8, f32[1024,384]{1,0:T(8,128)} %fusion.10, f32[1024,384]{1,0:T(8,128)} %fusion.12, f32[1024,384]{1,0:T(8,128)S(1)} %fusion.14, f32[1024,384]{1,0:T(8,128)} %fusion.16, f32[1024,384]{1,0:T(8,128)} %fusion.18, f32[1024,384]{1,0:T(8,128)S(1)} %fusion.20, ...), kind=kOutput, calls=%fused_computation.8 | convolution fusion | flops 312213504 | bytes 43548672 | tf_op jit(solution)/shard_map/dot_general | solution.py:43
  141.8 2.7 %fusion.3 = bf16[4,2,128,384]{3,2,1,0:T(8,128)(2,1)} fusion(f32[4,2,128,384]{3,2,1,0:T(8,128)} %bitcast.155, bf16[4,2,128,384]{3,2,1,0:T(8,128)(2,1)} %copy-done.3, f32[384]{0:T(512)S(1)} %copy-done.5), kind=kLoop, calls=%fused_computation.7 | loop fusion | flops 1572864 | bytes 3147264 | tf_op jit(solution)/shard_map/convert_element_type | solution.py:105
  (77 shorter events, 33.8 us)
Async XLA Ops:
  0.0 44.3 %copy-start = (bf16[3,3,3,16,384]{4,3,2,1,0:T(8,128)(2,1)S(1)}, bf16[3,3,3,16,384]{4,3,2,1,0:T(8,128)(2,1)}, u32[]{:S(2)}) copy-start(bf16[3,3,3,16,384]{4,3,2,1,0:T(8,128)(2,1)} %param.7) | copy-start | bytes 995332
  24.2 10.1 %collective-permute-start = (bf16[4,1,128,16]{2,3,1,0:T(8,128)(2,1)S(1)}, bf16[4,1,128,16]{2,3,1,0:T(8,128)(2,1)S(1)}, u32[]{:S(2)}, u32[]{:S(2)}) collective-permute-start(bf16[4,1,128,16]{2,3,1,0:T(8,128)(2,1)S(1)} %get-tuple-element.33), channel_id=1, source_target_pairs={{0,1},{1,2},{2,3},{3,4},{4,5},{5,6},{6,7},{7,8},{8,9},{9,10},{10,1... | collective-permute-start | bytes 49160 | tf_op jit(solution)/shard_map/ppermute | solution.py:15
  26.7 9.0 %collective-permute-start.1 = (bf16[4,1,128,16]{2,3,1,0:T(8,128)(2,1)S(1)}, bf16[4,1,128,16]{2,3,1,0:T(8,128)(2,1)S(1)}, u32[]{:S(2)}, u32[]{:S(2)}) collective-permute-start(bf16[4,1,128,16]{2,3,1,0:T(8,128)(2,1)S(1)} %get-tuple-element.34), channel_id=1, source_target_pairs={{1,0},{2,1},{3,2},{4,3},{5,4},{6,5},{7,6},{8,7},{9,8},{10,9},{11,1... | collective-permute-start | bytes 49160 | tf_op jit(solution)/shard_map/ppermute | solution.py:17
  35.7 8.6 %copy-start.6 = (f32[384]{0:T(512)S(1)}, f32[384]{0:T(512)}, u32[]{:S(2)}) copy-start(f32[384]{0:T(512)} %param.8) | copy-start | bytes 4612
  35.7 6.7 %collective-permute-start.2 = (bf16[2,4,128,16]{2,3,1,0:T(8,128)(2,1)S(1)}, bf16[2,4,128,16]{2,3,1,0:T(8,128)(2,1)S(1)}, u32[]{:S(2)}, u32[]{:S(2)}) collective-permute-start(bf16[2,4,128,16]{2,3,1,0:T(8,128)(2,1)S(1)} %pad_maximum_fusion.6), channel_id=1, source_target_pairs={{0,64},{64,128},{128,192},{1,65},{65,129},{129,193},{2,66},{66,130... | collective-permute-start | bytes 98312 | tf_op jit(solution)/shard_map/ppermute | solution.py:27
  43.9 1.3 copy-start.4
  44.3 19.6 %copy-start.2 = (bf16[3,3,3,384,384]{4,3,2,1,0:T(8,128)(2,1)S(1)}, bf16[3,3,3,384,384]{4,3,2,1,0:T(8,128)(2,1)}, u32[]{:S(2)}) copy-start(bf16[3,3,3,384,384]{4,3,2,1,0:T(8,128)(2,1)} %param.10) | copy-start | bytes 23887876
  45.2 0.9 copy-start.3
  46.0 14.4 %collective-permute-start.3 = (bf16[4,1,128,384]{3,2,1,0:T(8,128)(2,1)S(1)}, bf16[4,1,128,384]{3,2,1,0:T(8,128)(2,1)S(1)}, u32[]{:S(2)}, u32[]{:S(2)}) collective-permute-start(bf16[4,1,128,384]{3,2,1,0:T(8,128)(2,1)S(1)} %get-tuple-element.31), channel_id=1, source_target_pairs={{0,1},{1,2},{2,3},{3,4},{4,5},{5,6},{6,7},{7,8},{8,9},{9,10},{10,1... | collective-permute-start | bytes 1179656 | tf_op jit(solution)/shard_map/ppermute | solution.py:15
  48.2 13.7 %collective-permute-start.4 = (bf16[4,1,128,384]{3,2,1,0:T(8,128)(2,1)S(1)}, bf16[4,1,128,384]{3,2,1,0:T(8,128)(2,1)S(1)}, u32[]{:S(2)}, u32[]{:S(2)}) collective-permute-start(bf16[4,1,128,384]{3,2,1,0:T(8,128)(2,1)S(1)} %get-tuple-element.32), channel_id=1, source_target_pairs={{1,0},{2,1},{3,2},{4,3},{5,4},{6,5},{7,6},{8,7},{9,8},{10,9},{11,1... | collective-permute-start | bytes 1179656 | tf_op jit(solution)/shard_map/ppermute | solution.py:17
  62.0 14.8 %collective-permute-start.5 = (bf16[2,4,128,384]{3,2,1,0:T(8,128)(2,1)S(1)}, bf16[2,4,128,384]{3,2,1,0:T(8,128)(2,1)S(1)}, u32[]{:S(2)}, u32[]{:S(2)}) collective-permute-start(bf16[2,4,128,384]{3,2,1,0:T(8,128)(2,1)S(1)} %pad_maximum_fusion.2), channel_id=1, source_target_pairs={{0,64},{64,128},{128,192},{1,65},{65,129},{129,193},{2,66},{66,130... | collective-permute-start | bytes 2359304 | tf_op jit(solution)/shard_map/ppermute | solution.py:27
  126.9 14.9 %copy-start.5 = (f32[384]{0:T(512)S(1)}, f32[384]{0:T(512)}, u32[]{:S(2)}) copy-start(f32[384]{0:T(512)} %param.11) | copy-start | bytes 4612
  141.8 2.8 %copy-start.1 = (bf16[3,3,3,16,384]{4,3,2,1,0:T(8,128)(2,1)S(1)}, bf16[3,3,3,16,384]{4,3,2,1,0:T(8,128)(2,1)}, u32[]{:S(2)}) copy-start(bf16[3,3,3,16,384]{4,3,2,1,0:T(8,128)(2,1)} %param.7) | copy-start | bytes 995332
where the time goes:
time: 145 us
  matrix products  59.1 us (41%)
  starting transfers between devices  24.5 us (17%)
  blocking collectives  22.7 us (16%)
  waiting for transfers between devices  22.3 us (15%)
  local copies, waits for them, and re-layouts  11.6 us (8%)
  other arithmetic  4.04 us (3%)
    dot_general x27, matrix products, causal_conv(): jnp.dot(window.reshape(-1, window.shape[-1]), weight[tap_time, tap_row, t...  58.3 us
    all_to_all x1, blocking collectives, per_device(): lax.all_to_all(latent_tokens, 'space', split_axis=1, concat_axis=2, tiled...  22.7 us
    ppermute x2, starting transfers between devices, padded_2(): lax.ppermute(head, axis, [((i + 1) % count, i) for i in range(ends)])  16 us
    ppermute x2, waiting for transfers between devices, shifted(): lax.ppermute(value, axis, [(source, source + steps) for source in range(i...  15.6 us
    slice x3, local copies, waits for them, and re-layouts, causal_conv(): padded[tap_time:tap_time + frames, tap_row:tap_row + height, tap_col:tap_...  8.15 us
    ppermute x2, starting transfers between devices, padded_2(): lax.ppermute(tail, axis, [(i, (i + 1) % count) for i in range(ends)])  4.65 us
    ppermute x2, starting transfers between devices, shifted(): lax.ppermute(value, axis, [(source, source + steps) for source in range(i...  3.84 us
    ppermute x2, waiting for transfers between devices, padded_2(): lax.ppermute(tail, axis, [(i, (i + 1) % count) for i in range(ends)])  3.81 us
  transfers between devices with their start and end apart: 6, of which 5 were waited for; matrix products, arithmetic and copies ran while one was open for 1% of the time, Pallas kernels for 0%

commit v1 on v0

v1 whole, which is shorter than its diff:
```python
import functools

import jax
import jax.numpy as jnp
from jax import lax
from jax.experimental import pallas as pl
from jax.experimental.pallas import tpu as pltpu
from jax.sharding import PartitionSpec as P

MESH = pl.DeviceIdType.MESH
C = 384
LAT = 16
F32 = jnp.float32
BF16 = jnp.bfloat16


def exchange_kernel(tm_count, n, x_ref, r_ref, send_sem, recv_sem, send_next, recv_prev, own_sem):
    tm = lax.axis_index("tm")
    me = lax.axis_index("space")
    barrier = pltpu.get_barrier_semaphore()

    @pl.loop(1, n)
    def _(k):
        pl.semaphore_signal(barrier, inc=1, device_id=(tm, lax.rem(me + k, n)), device_id_type=MESH)

    @pl.when(tm > 0)
    def _():
        @pl.loop(0, n)
        def _(k):
            pl.semaphore_signal(barrier, inc=1, device_id=(tm - 1, lax.rem(me + k, n)), device_id_type=MESH)

    own = pltpu.make_async_copy(x_ref.at[pl.ds(me, 3)], r_ref.at[1, me], own_sem)
    own.start()

    @pl.when(tm == 0)
    def _():
        r_ref[0] = jnp.zeros(r_ref.shape[1:], r_ref.dtype)

    pl.semaphore_wait(barrier, n - 1 + n * (1 - tm // (tm_count - 1)))

    @pl.when(tm < tm_count - 1)
    def _():
        @pl.loop(0, n)
        def _(k):
            to = lax.rem(me + k, n)
            pltpu.make_async_remote_copy(
                src_ref=x_ref.at[pl.ds(to, 3)], dst_ref=r_ref.at[0, me],
                send_sem=send_next, recv_sem=recv_prev,
                device_id=(tm + 1, to), device_id_type=MESH,
            ).start()

    @pl.loop(1, n)
    def _(k):
        to = lax.rem(me + k, n)
        pltpu.make_async_remote_copy(
            src_ref=x_ref.at[pl.ds(to, 3)], dst_ref=r_ref.at[1, me],
            send_sem=send_sem, recv_sem=recv_sem,
            device_id=(tm, to), device_id_type=MESH,
        ).start()

    def await_all(half, count, sem):
        whole = r_ref.at[half, pl.ds(0, count)]
        pltpu.make_async_copy(whole, whole, sem).wait()

    own.wait()
    await_all(1, n - 1, send_sem)
    await_all(1, n - 1, recv_sem)

    @pl.when(tm < tm_count - 1)
    def _():
        await_all(0, n, send_next)

    @pl.when(tm > 0)
    def _():
        await_all(0, n, recv_prev)


def exchange(x, tm_count, n):
    return pl.pallas_call(
        functools.partial(exchange_kernel, tm_count, n),
        out_shape=jax.ShapeDtypeStruct((2, n, 3) + x.shape[1:], x.dtype),
        in_specs=[pl.BlockSpec(memory_space=pltpu.VMEM)],
        out_specs=pl.BlockSpec(memory_space=pltpu.VMEM),
        scratch_shapes=[pltpu.SemaphoreType.DMA] * 5,
        compiler_params=pltpu.CompilerParams(collective_id=0, has_side_effects=True),
        name="exchange",
    )(x)


def block_kernel(tm_count, n, g_ref, win_ref, bin_ref, gain_ref, w_ref, bmid_ref, out_ref, act, feat, tmp):
    cols = 64
    first_frames = lax.axis_index("tm") == 0
    me = lax.axis_index("space")
    bias = bin_ref[...]
    gain = gain_ref[...]
    for pair in range(2):
        lanes = slice(128 * pair, 128 * pair + 256)
        left = jnp.concatenate([g_ref[cols * a : cols * a + 6 * cols, lanes] for a in range(3)], axis=1)
        for row in range(2):
            rho = 2 * pair + row
            both = jnp.dot(left, win_ref[:, 2 * C * row : 2 * C * (row + 1)], preferred_element_type=F32)
            inside = True
            if rho == 0:
                inside = me > 0
            if rho == 3:
                inside = me < n - 1
            for parity in range(2):
                f = (both[:, C * parity : C * (parity + 1)] + bias).astype(BF16)
                if rho in (1, 2):
                    for frame in range(4):
                        feat[frame, rho - 1, parity] = f[cols * (frame + 2) : cols * (frame + 3)]
                v = f.astype(F32)
                scale = lax.rsqrt(jnp.mean(v * v, axis=-1, keepdims=True) + 1e-6)
                h = v * scale * (0.5 * gain)
                s = (h + h * jnp.tanh(h)).astype(BF16)
                for frame in range(6):
                    piece = s[cols * frame : cols * (frame + 1)]
                    keep = inside
                    if frame < 2:
                        keep = jnp.logical_and(keep, jnp.logical_not(first_frames))
                    if keep is not True:
                        piece = jnp.where(keep, piece, jnp.zeros_like(piece))
                    act[frame, rho, parity] = piece

    bmid = bmid_ref[...]

    @pl.loop(0, 4)
    def _(frame):
        lefts, rights = [], []
        for a in range(3):
            for b in range(3):
                lefts.append(act[frame + a, b : b + 2].reshape(4 * cols, C))
                rights.append(jnp.concatenate([w_ref[a, b, e] for e in range(3)], axis=1))
        sums = jnp.dot(
            jnp.concatenate(lefts, axis=1), jnp.concatenate(rights, axis=0), preferred_element_type=F32
        )
        edge = lax.broadcasted_iota(jnp.int32, (cols, C), 0)
        for y in range(2):
            even_in = sums[128 * y : 128 * y + 64]
            odd_in = sums[128 * y + 64 : 128 * y + 128]
            down = jnp.where(edge == 0, 0.0, pltpu.roll(odd_in[:, :C], 1, 0))
            up = jnp.where(edge == cols - 1, 0.0, pltpu.roll(even_in[:, 2 * C :], cols - 1, 0))
            even = down + even_in[:, C : 2 * C] + odd_in[:, 2 * C :]
            odd = even_in[:, :C] + odd_in[:, C : 2 * C] + up
            even = feat[frame, y, 0].astype(F32) + even + bmid
            odd = feat[frame, y, 1].astype(F32) + odd + bmid
            for k in range(3):
                ln = slice(128 * k, 128 * (k + 1))
                tmp[y, k, pl.ds(0, 64, stride=2), :] = even[:, ln]
                tmp[y, k, pl.ds(1, 64, stride=2), :] = odd[:, ln]
            for k in range(3):
                ln = slice(128 * k, 128 * (k + 1))
                out_ref[frame, y, :, ln] = tmp[y, k].astype(BF16)


def block(g, win, bin_, gain, w, bmid, tm_count, n):
    vm = pl.BlockSpec(memory_space=pltpu.VMEM)
    return pl.pallas_call(
        functools.partial(block_kernel, tm_count, n),
        out_shape=jax.ShapeDtypeStruct((4, 2, 128, C), BF16),
        in_specs=[vm] * 6,
        out_specs=vm,
        scratch_shapes=[
            pltpu.VMEM((6, 4, 2, 64, C), BF16),
            pltpu.VMEM((4, 2, 2, 64, C), BF16),
            pltpu.VMEM((2, 3, 128, 128), F32),
        ],
        compiler_params=pltpu.CompilerParams(vmem_limit_bytes=56 << 20),
        name="block",
    )(g, win, bin_, gain, w, bmid)


def spread_weight(w):
    zero = jnp.zeros_like(w)
    cols = jnp.concatenate([w, zero[:, :, :1]], 2), jnp.concatenate([zero[:, :, :1], w], 2)
    both = jnp.stack(cols, axis=4)
    pad = jnp.zeros_like(both[:, :1])
    rows = jnp.stack([jnp.concatenate([both, pad], 1), jnp.concatenate([pad, both], 1)], axis=4)
    return rows.reshape(3 * 4 * 4 * LAT, 4 * C)


def gather_columns(r):
    two, n, three = r.shape[:3]
    t = r.reshape(two, n, three, 2, 2, 2, 2, LAT).transpose(0, 3, 4, 1, 2, 5, 6, 7)
    t = t.reshape(8, n, 6, 2, LAT)
    before = jnp.pad(t[:, :-1, :, 1:], ((0, 0), (1, 0), (0, 0), (0, 0), (0, 0)))
    after = jnp.pad(t[:, 1:, :, :1], ((0, 0), (0, 1), (0, 0), (0, 0), (0, 0)))
    return jnp.concatenate([before, t, after], axis=3).reshape(8 * n, 6 * 4 * LAT)


def solution(mesh):
    tm_count, n = mesh.shape["tm"], mesh.shape["space"]

    def per_device(tokens, w_in, b_in, gain, w_mid, b_mid):
        x = tokens[:, :, 0].transpose(1, 0, 2).reshape(n, 2, 128)
        x = jnp.pad(x, ((1, 1), (0, 0), (0, 0)))
        r = exchange(x, tm_count, n)
        g = gather_columns(r)
        row = lambda v: v.reshape(1, C)
        return block(g, spread_weight(w_in), row(b_in), row(gain), w_mid, row(b_mid), tm_count, n)

    return jax.shard_map(
        per_device,
        mesh=mesh,
        in_specs=(P("tm", None, "space", None), P(), P(), P(), P(), P()),
        out_specs=P("tm", "space", None, None),
        check_vma=False,
    )
```

time: 145 us -> 52.9 us (0.36)
  the two profiles are of different devices: /device:TPU:6 before, /device:TPU:1 now
where the time goes in v1:
time: 52.9 us; the launch traced here: 52.7 us
  Pallas kernels  39.4 us (74%)
  local copies, waits for them, and re-layouts  12.6 us (24%)
  other arithmetic  0.6 us (1%)
    pallas_call x1, Pallas kernels, exchange(): pl.pallas_call(functools.partial(exchange_kernel, tm_count, n), out_shape...  21.7 us
    pallas_call x1, Pallas kernels, block(): pl.pallas_call(functools.partial(block_kernel, tm_count, n), out_shape=ja...  17.7 us
    reshape x1, local copies, waits for them, and re-layouts, spread_weight(): return rows.reshape(3 * 4 * 4 * LAT, 4 * C)  2.81 us
    another operation x2, local copies, waits for them, and re-layouts, spread_weight(): jnp.stack([jnp.concatenate([both, pad], 1), jnp.concatenate([pad, both],...  2.77 us
    reshape x3, local copies, waits for them, and re-layouts, per_device(): row = lambda v: v.reshape(1, C)  1.76 us
    reshape x2, local copies, waits for them, and re-layouts, gather_columns(): jnp.concatenate([before, t, after], axis=3).reshape(8 * n, 6 * 4 * LAT)  1.39 us
    another operation x1, local copies, waits for them, and re-layouts, spread_weight(): both = jnp.stack(cols, axis=4)  1.19 us
    pallas_call x1, local copies, waits for them, and re-layouts, exchange(): pl.pallas_call(functools.partial(exchange_kernel, tm_count, n), out_shape...  1.16 us

profile of v1, /device:TPU:1, one launch (start us, length us, event | category | flops | bytes accessed | tf_op | source)
XLA Modules:
  0.0 52.7 jit_solution(9177890708306790748)
XLA Ops:
  0.0 1.2 %pad_bitcast_fusion.3 = (bf16[3,3,4,16,1,384]{5,3,2,1,0,4:T(8,128)(2,1)S(1)}, bf16[3,3,4,16,1,384]{5,3,2,1,0,4:T(8,128)(2,1)S(1)}) fusion(bf16[3,3,3,16,384]{4,3,2,1,0:T(8,128)(2,1)} %param.7), kind=kLoop, calls=%fused_computation.11 | loop fusion | bytes 1216512 | tf_op jit(solution)/shard_map/stack | solution.py:176
  1.2 0.1 pad_maximum_fusion.1
  1.3 0.3 pad_bitcast_fusion.1
  1.7 0.3 pad_maximum_fusion
  1.9 2.4 %copy.18 = bf16[3,4,4,16,2,2,384]{6,5,4,3,2,1,0:T(2,128)(2,1)S(1)} copy(bf16[3,4,4,16,2,2,384]{6,3,2,1,0,5,4:T(8,128)(2,1)S(1)} %pad_maximum_fusion) | data formatting | bytes 4718592 | tf_op jit(solution)/shard_map/stack | solution.py:178
  4.4 0.0 copy-start
  4.4 2.8 %reshape.28.win_ref = bf16[768,1536]{1,0:T(8,128)(2,1)} reshape(bf16[3,4,4,16,2,2,384]{6,5,4,3,2,1,0:T(2,128)(2,1)S(1)} %copy.18) | data formatting | bytes 4718592 | tf_op jit(solution)/shard_map/reshape | solution.py:179
  7.2 0.1 copy.14
  7.3 0.1 reshape.24
  7.4 0.6 %pad.16.x_ref = bf16[66,2,128]{2,1,0:T(2,128)(2,1)} pad(bf16[64,2,128]{2,1,0:T(2,128)(2,1)S(1)} %reshape.24, bf16[]{:T(256)} %constant.1.clone.1), padding=1_1x0_0x0_0 | pad | bytes 66562 | tf_op jit(solution)/shard_map/jit(_pad)/pad | solution.py:196
  8.0 21.7 %exchange.1 = bf16[2,64,3,2,128]{4,3,2,1,0:T(2,128)(2,1)} custom-call(bf16[66,2,128]{2,1,0:T(2,128)(2,1)} %pad.16.x_ref), custom_call_target="tpu_custom_call" | custom-call | tf_op jit(solution)/shard_map/exchange/pallas_call | solution.py:79
  29.7 1.2 %copy.15 = bf16[2,64,3,2,128]{1,4,3,2,0:T(8,128)(2,1)S(1)} copy(bf16[2,64,3,2,128]{4,3,2,1,0:T(2,128)(2,1)} %exchange.1) | data formatting | bytes 393216 | tf_op jit(solution)/shard_map/exchange/pallas_call | solution.py:79
  30.9 0.1 fusion.4
  31.0 0.2 fusion.2
  31.3 0.0 copy-start.1
  31.3 0.0 copy-start.2
  31.3 0.0 copy-start.3
  31.3 0.5 copy.17
  31.8 0.5 reshape.27
  32.3 0.9 %copy.19.g_ref = bf16[512,384]{1,0:T(8,128)(2,1)} copy(bf16[512,384]{0,1:T(8,128)(2,1)S(1)} %reshape.27) | data formatting | bytes 786432 | tf_op jit(solution)/shard_map/reshape | solution.py:188
  33.2 0.6 %reshape.29.bin_ref = f32[1,384]{1,0:T(1,128)} reshape(f32[384]{0:T(512)S(1)} %copy-done.1) | data formatting | bytes 3072 | tf_op jit(solution)/shard_map/reshape | solution.py:199
  33.8 0.6 %reshape.30.gain_ref = f32[1,384]{1,0:T(1,128)} reshape(f32[384]{0:T(512)S(1)} %copy-done.2) | data formatting | bytes 3072 | tf_op jit(solution)/shard_map/reshape | solution.py:199
  34.4 0.6 %reshape.31.bmid_ref = f32[1,384]{1,0:T(1,128)} reshape(f32[384]{0:T(512)S(1)} %copy-done.3) | data formatting | bytes 3072 | tf_op jit(solution)/shard_map/reshape | solution.py:199
  35.0 17.7 %block.1 = bf16[4,2,128,384]{3,2,1,0:T(8,128)(2,1)} custom-call(bf16[512,384]{1,0:T(8,128)(2,1)} %copy.19.g_ref, bf16[768,1536]{1,0:T(8,128)(2,1)} %reshape.28.win_ref, f32[1,384]{1,0:T(1,128)} %reshape.29.bin_ref, f32[1,384]{1,0:T(1,128)} %reshape.30.gain_ref, bf16[3,3,3,384,384]{4,3,2,1,0:T(8,128)(2,1)} %w_ref.1, f32[1,384]{1,0:T(1,128)} %reshape.31.bmid_ref), custom_call_target="tpu_custom_call" | custom-call | tf_op jit(solution)/shard_map/block/pallas_call | solution.py:158
  (5 shorter events, 0.0 us)
Async XLA Ops:
  4.4 2.8 %copy-start = (bf16[4,64,1,64]{3,1,2,0:T(8,128)(2,1)S(1)}, bf16[4,64,1,64]{3,1,2,0:T(8,128)(2,1)}, u32[]{:S(2)}) copy-start(bf16[4,64,1,64]{3,1,2,0:T(8,128)(2,1)} %param.6) | copy-start | bytes 98308
  31.3 2.0 %copy-start.1 = (f32[384]{0:T(512)S(1)}, f32[384]{0:T(512)}, u32[]{:S(2)}) copy-start(f32[384]{0:T(512)} %param.8) | copy-start | bytes 4612
  31.3 2.5 %copy-start.2 = (f32[384]{0:T(512)S(1)}, f32[384]{0:T(512)}, u32[]{:S(2)}) copy-start(f32[384]{0:T(512)} %param.9) | copy-start | bytes 4612
  31.3 3.1 %copy-start.3 = (f32[384]{0:T(512)S(1)}, f32[384]{0:T(512)}, u32[]{:S(2)}) copy-start(f32[384]{0:T(512)} %param.11) | copy-start | bytes 4612

commit v2 on v1

v2 whole, which is shorter than its diff:
```python
import functools

import jax
import jax.numpy as jnp
from jax import lax
from jax.experimental import pallas as pl
from jax.experimental.pallas import tpu as pltpu
from jax.sharding import PartitionSpec as P

MESH = pl.DeviceIdType.MESH
C = 384
LAT = 16
COLS = 64
F32 = jnp.float32
BF16 = jnp.bfloat16
SPACE = (2, 4, 8)


def far_first():
    def hops(step):
        return sum(min(d, size - d) for d, size in zip(step, SPACE))

    steps = [(i, j, k) for i in range(SPACE[0]) for j in range(SPACE[1]) for k in range(SPACE[2])]
    return sorted(steps, key=hops, reverse=True)


def exchange_kernel(
    tm_count, n, tok_hbm, w_in_hbm, w_hbm, r_ref, win_ref, pick_ref, w_ref, u_ref,
    tok, x, w_in, send_sem, recv_sem, send_next, recv_prev, own_sem, tok_sem, w_in_sem, w_sem,
):
    tm = lax.axis_index("tm")
    me = lax.axis_index("space")
    copies = (
        pltpu.make_async_copy(tok_hbm, tok, tok_sem),
        pltpu.make_async_copy(w_in_hbm, w_in, w_in_sem),
        pltpu.make_async_copy(w_hbm, w_ref, w_sem),
    )
    for copy in copies:
        copy.start()

    _, ny, nz = SPACE
    place = (me // (ny * nz), (me // nz) % ny, me % nz)
    strides = (ny * nz, nz, 1)
    along = [[((place[d] + s) % SPACE[d]) * strides[d] for s in range(SPACE[d])] for d in range(3)]
    peers = [along[0][i] + along[1][j] + along[2][k] for i, j, k in far_first()]

    barrier = pltpu.get_barrier_semaphore()

    @pl.when(tm > 0)
    def _():
        for peer in peers:
            pl.semaphore_signal(barrier, inc=1, device_id=(tm - 1, peer), device_id_type=MESH)

    copies[0].wait()
    for h in range(2):
        x[:, h, :] = jnp.concatenate([tok[2 * h], tok[2 * h + 1]], axis=1)

    for peer in peers[:-1]:
        pl.semaphore_signal(barrier, inc=1, device_id=(tm, peer), device_id_type=MESH)

    @pl.when(tm == 0)
    def _():
        r_ref[0] = jnp.zeros(r_ref.shape[1:], r_ref.dtype)

    def rows_for(peer):
        return x.at[pl.ds(jnp.clip(peer - 1, 0, n - 3), 3)]

    pl.semaphore_wait(barrier, n - 1 + n * (1 - tm // (tm_count - 1)))
    own = pltpu.make_async_copy(rows_for(me), r_ref.at[1, me], own_sem)
    own.start()

    @pl.when(tm < tm_count - 1)
    def _():
        for peer in peers:
            pltpu.make_async_remote_copy(
                src_ref=rows_for(peer), dst_ref=r_ref.at[0, me], send_sem=send_next, recv_sem=recv_prev,
                device_id=(tm + 1, peer), device_id_type=MESH,
            ).start()

    for peer in peers[:-1]:
        pltpu.make_async_remote_copy(
            src_ref=rows_for(peer), dst_ref=r_ref.at[1, me], send_sem=send_sem, recv_sem=recv_sem,
            device_id=(tm, peer), device_id_type=MESH,
        ).start()

    copies[1].wait()
    win_ref[...] = jnp.zeros(win_ref.shape, BF16)
    for a in range(3):
        for b in range(3):
            block = w_in[a, b].reshape(3 * LAT, C)
            for row in range(2):
                for parity in range(2):
                    start = ((a * 4 + b + row) * 4 + parity) * LAT
                    lanes = slice((2 * row + parity) * C, (2 * row + parity + 1) * C)
                    win_ref[start : start + 3 * LAT, lanes] = block

    lane = lax.broadcasted_iota(jnp.int32, (C, C), 1)
    have = lax.broadcasted_iota(jnp.int32, (C, C), 0)
    y, col, c = lane // 64, (lane // 16) % 4, lane % 16
    shift = jnp.where(me == 0, -1, jnp.where(me == n - 1, 1, 0))
    want = (y // 2 + shift) * 128 + (y % 2) * 32 + ((col + 1) % 2) * 16 + c
    for fp in range(2):
        pick_ref[:, C * fp : C * (fp + 1)] = jnp.where(have == want + 64 * fp, 1.0, 0.0).astype(BF16)

    copies[2].wait()

    @pl.loop(0, 9)
    def _(i):
        a, e = i // 3, i % 3
        for part in range(3):
            rows = slice(128 * part, 128 * (part + 1))
            outer = 0.5 * (w_ref[a, 0, e, rows].astype(F32) + w_ref[a, 2, e, rows].astype(F32))
            inner = 0.5 * w_ref[a, 1, e, rows].astype(F32)
            u_ref[0, a, e, rows] = (outer + inner).astype(BF16)
            u_ref[1, a, e, rows] = (outer - inner).astype(BF16)

    def await_all(half, count, sem):
        whole = r_ref.at[half, pl.ds(0, count)]
        pltpu.make_async_copy(whole, whole, sem).wait()

    own.wait()
    await_all(1, n - 1, send_sem)
    await_all(1, n - 1, recv_sem)

    @pl.when(tm < tm_count - 1)
    def _():
        await_all(0, n, send_next)

    @pl.when(tm > 0)
    def _():
        await_all(0, n, recv_prev)


def exchange(tok, w_in, w, tm_count, n):
    hbm = pl.BlockSpec(memory_space=pltpu.HBM)
    vm = pl.BlockSpec(memory_space=pltpu.VMEM)
    return pl.pallas_call(
        functools.partial(exchange_kernel, tm_count, n),
        out_shape=(
            jax.ShapeDtypeStruct((2, n, 3, 2, 128), BF16),
            jax.ShapeDtypeStruct((3 * 4 * 4 * LAT, 4 * C), BF16),
            jax.ShapeDtypeStruct((C, 2 * C), BF16),
            jax.ShapeDtypeStruct(w.shape, BF16),
            jax.ShapeDtypeStruct((2, 3, 3, C, C), BF16),
        ),
        in_specs=[hbm] * 3,
        out_specs=[vm] * 5,
        scratch_shapes=[
            pltpu.VMEM(tok.shape, BF16),
            pltpu.VMEM((n, 2, 128), BF16),
            pltpu.VMEM(w_in.shape, BF16),
        ]
        + [pltpu.SemaphoreType.DMA] * 8,
        compiler_params=pltpu.CompilerParams(collective_id=0, has_side_effects=True, vmem_limit_bytes=24 << 20),
        name="exchange",
    )(*(pltpu.with_memory_space_constraint(v, pltpu.HBM) for v in (tok, w_in, w)))


def block_kernel(
    tm_count, n, r_ref, win_ref, pick_ref, w_ref, u_ref, bin_ref, gain_ref, bmid_ref, out_ref, g, act, d, feat, part, tmp
):
    first_frames = lax.axis_index("tm") == 0
    me = lax.axis_index("space")

    sub = lax.broadcasted_iota(jnp.int32, (COLS, C), 0)
    col = (lax.broadcasted_iota(jnp.int32, (COLS, C), 1) // 16) % 4
    came = jnp.concatenate(
        [
            jnp.concatenate([r_ref[tb, :, t, h, :] for t in range(3)], axis=1)
            for tb in range(2)
            for h in range(2)
        ],
        axis=0,
    )
    laid = jnp.dot(came, pick_ref[...], preferred_element_type=F32)
    for k in range(4):
        for fp in range(2):
            here = laid[COLS * k : COLS * (k + 1), C * fp : C * (fp + 1)]
            before = jnp.where(sub == 0, 0.0, pltpu.roll(here, 1, 0))
            after = jnp.where(sub == COLS - 1, 0.0, pltpu.roll(here, COLS - 1, 0))
            g[2 * k + fp] = jnp.where(col == 0, before, jnp.where(col == 3, after, here)).astype(BF16)

    bias = bin_ref[...].reshape(1, C)
    half_gain = 0.5 * gain_ref[...].reshape(1, C)
    for pair in range(2):
        lanes = slice(128 * pair, 128 * pair + 256)
        left = jnp.concatenate([g[a : a + 6, :, lanes].reshape(6 * COLS, 256) for a in range(3)], axis=1)
        rows = []
        for row in range(2):
            rho = 2 * pair + row
            both = jnp.dot(left, win_ref[:, 2 * C * row : 2 * C * (row + 1)], preferred_element_type=F32)
            inside = True
            if rho == 0:
                inside = me > 0
            if rho == 3:
                inside = me < n - 1
            for parity in range(2):
                for frame in range(6):
                    f = both[COLS * frame : COLS * (frame + 1), C * parity : C * (parity + 1)]
                    f = (f + bias).astype(BF16)
                    if rho in (1, 2) and frame >= 2:
                        feat[frame - 2, rho - 1, parity] = f
                    v = f.astype(F32)
                    scale = lax.rsqrt(jnp.mean(v * v, axis=-1, keepdims=True) + 1e-6)
                    half = v * scale * half_gain
                    s = half + half * jnp.tanh(half)
                    keep = inside
                    if frame < 2:
                        keep = jnp.logical_and(keep, jnp.logical_not(first_frames))
                    if keep is not True:
                        s = jnp.where(keep, s, 0.0)
                    s = s.astype(BF16)
                    at = pl.ds(128 * frame + COLS * parity, COLS)
                    if rho < 2:
                        act[rho, frame, parity] = s
                    elif rho == 2:
                        a0 = act[0, frame, parity].astype(F32)
                        a1 = act[1, frame, parity].astype(F32)
                        s = s.astype(F32)
                        d[0, at] = (a0 - s).astype(BF16)
                        d[1, at] = (a1 + s).astype(BF16)
                        d[2, at] = (s - a1).astype(BF16)
                    else:
                        a1 = act[1, frame, parity].astype(F32)
                        d[3, at] = (a1 - s.astype(F32)).astype(BF16)

    bmid = bmid_ref[...].reshape(1, C)
    edge = lax.broadcasted_iota(jnp.int32, (COLS, 128), 0)
    cells = [(k, e) for k in range(3) for e in range(3)]

    def weight(eta, a, k, e):
        lanes = slice(128 * k, 128 * (k + 1))
        if eta == 0:
            return w_ref[a, 0, e, :, lanes]
        if eta == 3:
            return w_ref[a, 2, e, :, lanes]
        return u_ref[eta - 1, a, e, :, lanes]

    done = 0
    for tile in range(5):
        here = cells[2 * tile : 2 * tile + 2]
        m = []
        for eta in range(4):
            left = jnp.concatenate([d[eta, 128 * a : 128 * a + 512] for a in range(3)], axis=1)
            right = jnp.concatenate(
                [jnp.concatenate([weight(eta, a, k, e) for k, e in here], axis=1) for a in range(3)], axis=0
            )
            m.append(jnp.dot(left, right, preferred_element_type=F32))
        lanes = slice(256 * tile, 256 * tile + 128 * len(here))
        part[0, :, lanes] = (m[1] + m[2]) + m[0]
        part[1, :, lanes] = (m[1] - m[2]) - m[3]
        while done < 3 and 3 * (done + 1) <= 2 * tile + len(here):
            k = done
            done += 1
            ln = slice(128 * k, 128 * (k + 1))
            by_tap = [slice(128 * (3 * k + e), 128 * (3 * k + e + 1)) for e in range(3)]
            for frame in range(4):
                at_even = slice(128 * frame, 128 * frame + COLS)
                at_odd = slice(128 * frame + COLS, 128 * (frame + 1))
                for yy in range(2):
                    down = jnp.where(edge == 0, 0.0, pltpu.roll(part[yy, at_odd, by_tap[0]], 1, 0))
                    up = jnp.where(edge == COLS - 1, 0.0, pltpu.roll(part[yy, at_even, by_tap[2]], COLS - 1, 0))
                    even = down + part[yy, at_even, by_tap[1]] + part[yy, at_odd, by_tap[2]]
                    odd = part[yy, at_even, by_tap[0]] + part[yy, at_odd, by_tap[1]] + up
                    even = feat[frame, yy, 0, :, ln].astype(F32) + even + bmid[:, ln]
                    odd = feat[frame, yy, 1, :, ln].astype(F32) + odd + bmid[:, ln]
                    tmp[k, frame, yy, pl.ds(0, COLS, stride=2), :] = even
                    tmp[k, frame, yy, pl.ds(1, COLS, stride=2), :] = odd
                    out_ref[frame, yy, :, ln] = tmp[k, frame, yy].astype(BF16)


def block(r, win, pick, w, u, b_in, gain, b_mid, tm_count, n):
    vm = pl.BlockSpec(memory_space=pltpu.VMEM)
    return pl.pallas_call(
        functools.partial(block_kernel, tm_count, n),
        out_shape=jax.ShapeDtypeStruct((4, 2, 2 * COLS, C), BF16),
        in_specs=[vm] * 8,
        out_specs=vm,
        scratch_shapes=[
            pltpu.VMEM((8, COLS, C), BF16),
            pltpu.VMEM((2, 6, 2, COLS, C), BF16),
            pltpu.VMEM((4, 6 * 128, C), BF16),
            pltpu.VMEM((4, 2, 2, COLS, C), BF16),
            pltpu.VMEM((2, 512, 3 * C), F32),
            pltpu.VMEM((3, 4, 2, 128, 128), F32),
        ],
        compiler_params=pltpu.CompilerParams(vmem_limit_bytes=24 << 20),
        name="block",
    )(r, win, pick, w, u, b_in, gain, b_mid)


def solution(mesh):
    tm_count, n = mesh.shape["tm"], mesh.shape["space"]

    def per_device(tokens, w_in, b_in, gain, w_mid, b_mid):
        r, win, pick, w, u = exchange(tokens[:, :, 0], w_in, w_mid, tm_count, n)
        return block(r, win, pick, w, u, b_in, gain, b_mid, tm_count, n)

    return jax.shard_map(
        per_device,
        mesh=mesh,
        in_specs=(P("tm", None, "space", None), P(), P(), P(), P(), P()),
        out_specs=P("tm", "space", None, None),
        check_vma=False,
    )
```

time: 52.9 us -> 31.7 us (0.60)
  local copies, waits for them, and re-layouts: 12.6 us -> 0.01 us
  Pallas kernels: 39.4 us -> 31.6 us
  other arithmetic: 0.6 us -> 0 us
    pallas_call x1, Pallas kernels: 17.7 us -> 11.5 us  [block(): pl.pallas_call(functools.partial(block_kernel, tm_count, n), out_shape=ja...]
    reshape x7 -> x0, local copies, waits for them, and re-layouts: 6.06 us -> none  [the longest x1 2.81 us: spread_weight(): return rows.reshape(3 * 4 * 4 * LAT, 4 * C)]
    another operation x3 -> x0, local copies, waits for them, and re-layouts: 3.96 us -> none  [the longest x2 2.77 us: spread_weight(): jnp.stack([jnp.concatenate([both, pad], 1), jnp.concatenate([pad, both],...]
    pallas_call x1, Pallas kernels: 21.7 us -> 20 us  [exchange(): pl.pallas_call(functools.partial(exchange_kernel, tm_count, n), out_shape...]
    pallas_call x1 -> x0, local copies, waits for them, and re-layouts: 1.16 us -> none  [exchange(): pl.pallas_call(functools.partial(exchange_kernel, tm_count, n), out_shape...]
    pad x1 -> x0, local copies, waits for them, and re-layouts: 0.65 us -> none  [per_device(): x = jnp.pad(x, ((1, 1), (0, 0), (0, 0)))]
where the time goes in v2:
time: 31.7 us; the launch traced here: 31.6 us
  Pallas kernels  31.6 us (100%)
    pallas_call x1, Pallas kernels, exchange(): pl.pallas_call(functools.partial(exchange_kernel, tm_count, n), out_shape...  20 us
    pallas_call x1, Pallas kernels, block(): pl.pallas_call(functools.partial(block_kernel, tm_count, n), out_shape=ja...  11.5 us

profile of v2, /device:TPU:1, one launch (start us, length us, event | category | flops | bytes accessed | tf_op | source)
XLA Modules:
  0.0 31.6 jit_solution(6562680757806131227)
XLA Ops:
  0.0 0.0 copy-start.2
  0.0 0.0 copy-start.1
  0.0 0.0 copy-start
  0.0 20.0 %exchange.1 = (bf16[2,64,3,2,128]{4,3,2,1,0:T(2,128)(2,1)S(1)}, bf16[768,1536]{1,0:T(8,128)(2,1)S(1)}, bf16[384,768]{1,0:T(8,128)(2,1)S(1)}, bf16[3,3,3,384,384]...) custom-call(bf16[4,64,64]{2,1,0:T(8,128)(2,1)} %bitcast.1, bf16[3,3,3,16,384]{4,3,2,1,0:T(8,128)(2,1)} %w_in_hbm.1, ...), custom_call_target="tpu_custom_call" | custom-call | tf_op jit(solution)/shard_map/exchange/pallas_call | solution.py:137
  20.0 0.0 copy-done.2
  20.0 0.0 copy-done.1
  20.0 0.0 copy-done
  20.1 11.5 %block.1 = bf16[4,2,128,384]{3,2,1,0:T(8,128)(2,1)} custom-call(bf16[2,64,3,2,128]{4,3,2,1,0:T(2,128)(2,1)S(1)} %get-tuple-element.10.r_ref, bf16[768,1536]{1,0:T(8,128)(2,1)S(1)} %get-tuple-element.11.win_ref, bf16[384,768]{1,0:T(8,128)(2,1)S(1)} %get-tuple-element.12.pick_ref, bf16[3,3,3,384,384]{4,3,2,1,0:T(8,128)(2,1)S(1)} %get-tuple-element.13.w_ref, ...), custom_call_target="tpu_custom_call" | custom-call | tf_op jit(solution)/shard_map/block/pallas_call | solution.py:274
Async XLA Ops:
  0.0 20.0 %copy-start.2 = (f32[384]{0:T(512)S(1)}, f32[384]{0:T(512)}, u32[]{:S(2)}) copy-start(f32[384]{0:T(512)} %bmid_ref.1) | copy-start | bytes 4612
  0.0 20.0 %copy-start.1 = (f32[384]{0:T(512)S(1)}, f32[384]{0:T(512)}, u32[]{:S(2)}) copy-start(f32[384]{0:T(512)} %gain_ref.1) | copy-start | bytes 4612
  0.0 20.0 %copy-start = (f32[384]{0:T(512)S(1)}, f32[384]{0:T(512)}, u32[]{:S(2)}) copy-start(f32[384]{0:T(512)} %bin_ref.1) | copy-start | bytes 4612

commit v3 on v2

v3 whole, which is shorter than its diff:
```python
import functools

import jax
import jax.numpy as jnp
from jax import lax
from jax.experimental import pallas as pl
from jax.experimental.pallas import tpu as pltpu
from jax.sharding import PartitionSpec as P

MESH = pl.DeviceIdType.MESH
C = 384
LAT = 16
COLS = 64
F32 = jnp.float32
BF16 = jnp.bfloat16
SPACE = (2, 4, 8)


def far_first():
    def hops(step):
        return sum(min(d, size - d) for d, size in zip(step, SPACE))

    steps = [(i, j, k) for i in range(SPACE[0]) for j in range(SPACE[1]) for k in range(SPACE[2])]
    return sorted(steps, key=hops, reverse=True)


def lay_out_columns(r_ref, tb, pick_ref, spread, g, first):
    came = jnp.concatenate([r_ref[tb, t].reshape(2 * COLS, 128) for t in range(3)], axis=1)
    laid = jnp.dot(came, pick_ref[...], preferred_element_type=F32)
    spread[:, 0:8, :] = jnp.zeros((6, 8, 128), F32)
    spread[:, 136:144, :] = jnp.zeros((6, 8, 128), F32)
    for k in range(6):
        spread[k, 8:136, :] = laid[:, 128 * k : 128 * (k + 1)]
    col = (lax.broadcasted_iota(jnp.int32, (COLS, 128), 1) // 16) % 4
    for h in range(2):
        for fp in range(2):
            for q in range(3):
                before, here, after = (
                    spread[3 * fp + q, pl.ds(8 + h + 2 * step, COLS, stride=2), :] for step in (-1, 0, 1)
                )
                both = jnp.where(col == 0, before, jnp.where(col == 3, after, here))
                g[first + 2 * h + fp, :, 128 * q : 128 * (q + 1)] = both.astype(BF16)


def first_products(frames, count, win_ref):
    both = []
    for pair in range(2):
        lanes = slice(128 * pair, 128 * pair + 256)
        left = jnp.concatenate([frames(a, lanes) for a in range(3)], axis=1)
        for row in range(2):
            both.append(
                jnp.dot(left, win_ref[:, 2 * C * row : 2 * C * (row + 1)], preferred_element_type=F32)
            )
    return both


def activate(both, sub, bias, half_gain, keeps, feat, d):
    for parity in range(2):
        for block_row in range(COLS // 16):
            rows = slice(COLS * sub + 16 * block_row, COLS * sub + 16 * (block_row + 1))
            s = []
            for rho in range(4):
                f = (both[rho][rows, C * parity : C * (parity + 1)] + bias).astype(BF16)
                if rho in (1, 2) and feat is not None:
                    feat[rho - 1, parity, 16 * block_row : 16 * (block_row + 1)] = f
                v = f.astype(F32)
                scale = lax.rsqrt(jnp.sum(v * v, axis=-1, keepdims=True) * (1.0 / C) + 1e-6)
                if keeps[rho] is not None:
                    scale = scale * keeps[rho]
                half = v * scale * half_gain
                s.append(half + half * jnp.tanh(half))
            start = 128 * sub + COLS * parity + 16 * block_row
            at = slice(start, start + 16)
            d[0, at] = (s[0] - s[2]).astype(BF16)
            d[1, at] = (s[1] + s[2]).astype(BF16)
            d[2, at] = (s[2] - s[1]).astype(BF16)
            d[3, at] = (s[1] - s[3]).astype(BF16)


def edges(n):
    me = lax.axis_index("space")
    return jnp.where(me == 0, 0.0, 1.0), None, None, jnp.where(me == n - 1, 0.0, 1.0)


def exchange_kernel(
    tm_count, n, tok_hbm, w_in_hbm, w_hbm, bin_hbm, gain_hbm,
    r_ref, win_ref, pick_ref, w_ref, u_ref, g_ref, feat_ref, d_ref,
    tok, x, w_in, bin_ref, gain_ref, spread,
    send_sem, recv_sem, send_next, recv_prev, own_sem, tok_sem, w_in_sem, bin_sem, gain_sem, w_sem,
):
    tm = lax.axis_index("tm")
    me = lax.axis_index("space")
    copies = (
        pltpu.make_async_copy(tok_hbm, tok, tok_sem),
        pltpu.make_async_copy(w_in_hbm, w_in, w_in_sem),
        pltpu.make_async_copy(bin_hbm, bin_ref, bin_sem),
        pltpu.make_async_copy(gain_hbm, gain_ref, gain_sem),
        pltpu.make_async_copy(w_hbm, w_ref, w_sem),
    )
    for copy in copies:
        copy.start()

    _, ny, nz = SPACE
    place = (me // (ny * nz), (me // nz) % ny, me % nz)
    strides = (ny * nz, nz, 1)
    along = [[((place[d] + s) % SPACE[d]) * strides[d] for s in range(SPACE[d])] for d in range(3)]
    peers = [along[0][i] + along[1][j] + along[2][k] for i, j, k in far_first()]

    barrier = pltpu.get_barrier_semaphore()

    def signal(group):
        for peer in group:
            if peer is not peers[-1]:
                pl.semaphore_signal(barrier, inc=1, device_id=(tm, peer), device_id_type=MESH)

        @pl.when(tm > 0)
        def _():
            for peer in group:
                pl.semaphore_signal(barrier, inc=1, device_id=(tm - 1, peer), device_id_type=MESH)

    signal(peers[:40])
    copies[0].wait()
    for h in range(2):
        x[:, h, :] = jnp.concatenate([tok[2 * h], tok[2 * h + 1]], axis=1)
    signal(peers[40:])

    @pl.when(tm == 0)
    def _():
        r_ref[0] = jnp.zeros(r_ref.shape[1:], r_ref.dtype)

    def rows_for(peer):
        return x.at[pl.ds(jnp.clip(peer - 1, 0, n - 3), 3)]

    pl.semaphore_wait(barrier, n - 1 + n * (1 - tm // (tm_count - 1)))
    own = pltpu.make_async_copy(rows_for(me), r_ref.at[1, :, me], own_sem)
    own.start()

    for peer in peers[:-1]:
        pltpu.make_async_remote_copy(
            src_ref=rows_for(peer), dst_ref=r_ref.at[1, :, me], send_sem=send_sem, recv_sem=recv_sem,
            device_id=(tm, peer), device_id_type=MESH,
        ).start()

    @pl.when(tm < tm_count - 1)
    def _():
        for peer in peers:
            pltpu.make_async_remote_copy(
                src_ref=rows_for(peer), dst_ref=r_ref.at[0, :, me], send_sem=send_next, recv_sem=recv_prev,
                device_id=(tm + 1, peer), device_id_type=MESH,
            ).start()

    copies[1].wait()
    win_ref[...] = jnp.zeros(win_ref.shape, BF16)
    for a in range(3):
        for b in range(3):
            block = w_in[a, b].reshape(3 * LAT, C)
            for row in range(2):
                for parity in range(2):
                    start = ((a * 4 + b + row) * 4 + parity) * LAT
                    lanes = slice((2 * row + parity) * C, (2 * row + parity + 1) * C)
                    win_ref[start : start + 3 * LAT, lanes] = block

    lane = lax.broadcasted_iota(jnp.int32, (C, C), 1)
    have = lax.broadcasted_iota(jnp.int32, (C, C), 0)
    y, col, c = lane // 64, (lane // 16) % 4, lane % 16
    shift = jnp.where(me == 0, -1, jnp.where(me == n - 1, 1, 0))
    want = (y // 2 + shift) * 128 + (y % 2) * 32 + ((col + 1) % 2) * 16 + c
    for fp in range(2):
        pick_ref[:, C * fp : C * (fp + 1)] = jnp.where(have == want + 64 * fp, 1.0, 0.0).astype(BF16)

    copies[4].wait()

    @pl.loop(0, 9)
    def _(i):
        a, e = i // 3, i % 3
        for part in range(3):
            rows = slice(128 * part, 128 * (part + 1))
            outer = 0.5 * (w_ref[a, 0, e, rows].astype(F32) + w_ref[a, 2, e, rows].astype(F32))
            inner = 0.5 * w_ref[a, 1, e, rows].astype(F32)
            u_ref[0, a, e, rows] = (outer + inner).astype(BF16)
            u_ref[1, a, e, rows] = (outer - inner).astype(BF16)

    def await_all(half, count, sem):
        whole = r_ref.at[half, :, pl.ds(0, count)]
        pltpu.make_async_copy(whole, whole, sem).wait()

    own.wait()
    await_all(1, n - 1, recv_sem)

    copies[2].wait()
    copies[3].wait()
    lay_out_columns(r_ref, 1, pick_ref, spread, g_ref, 0)
    both = first_products(
        lambda a, lanes: g_ref[a : a + 2, :, lanes].reshape(2 * COLS, 256), 2, win_ref
    )
    bias = bin_ref[...].reshape(1, C)
    half_gain = 0.5 * gain_ref[...].reshape(1, C)
    for sub in range(2):
        activate(both, sub, bias, half_gain, edges(n), feat_ref.at[sub], d_ref)

    await_all(1, n - 1, send_sem)

    @pl.when(tm < tm_count - 1)
    def _():
        await_all(0, n, send_next)

    @pl.when(tm > 0)
    def _():
        await_all(0, n, recv_prev)


def exchange(tok, w_in, w, b_in, gain, tm_count, n):
    hbm = pl.BlockSpec(memory_space=pltpu.HBM)
    vm = pl.BlockSpec(memory_space=pltpu.VMEM)
    return pl.pallas_call(
        functools.partial(exchange_kernel, tm_count, n),
        out_shape=(
            jax.ShapeDtypeStruct((2, 3, n, 2, 128), BF16),
            jax.ShapeDtypeStruct((3 * 4 * 4 * LAT, 4 * C), BF16),
            jax.ShapeDtypeStruct((C, 2 * C), BF16),
            jax.ShapeDtypeStruct(w.shape, BF16),
            jax.ShapeDtypeStruct((2, 3, 3, C, C), BF16),
            jax.ShapeDtypeStruct((4, COLS, C), BF16),
            jax.ShapeDtypeStruct((2, 2, 2, COLS, C), BF16),
            jax.ShapeDtypeStruct((4, 2 * 128, C), BF16),
        ),
        in_specs=[hbm] * 5,
        out_specs=[vm] * 8,
        scratch_shapes=[
            pltpu.VMEM(tok.shape, BF16),
            pltpu.VMEM((n, 2, 128), BF16),
            pltpu.VMEM(w_in.shape, BF16),
            pltpu.VMEM((C,), F32),
            pltpu.VMEM((C,), F32),
            pltpu.VMEM((6, 2 * COLS + 16, 128), F32),
        ]
        + [pltpu.SemaphoreType.DMA] * 10,
        compiler_params=pltpu.CompilerParams(collective_id=0, has_side_effects=True, vmem_limit_bytes=24 << 20),
        name="exchange",
    )(*(pltpu.with_memory_space_constraint(v, pltpu.HBM) for v in (tok, w_in, w, b_in, gain)))


def block_kernel(
    tm_count, n, r_ref, win_ref, pick_ref, w_ref, u_ref, own_g, own_feat, own_d, bin_ref, gain_ref, bmid_ref,
    out_ref, spread, g, d, feat, part, down, up, tmp, made, out_sem,
):
    down[:, :, :, 0:8, :] = jnp.zeros(down.shape[:3] + (8, 128), F32)
    up[:, :, :, COLS : COLS + 8, :] = jnp.zeros(up.shape[:3] + (8, 128), F32)
    lay_out_columns(r_ref, 0, pick_ref, spread, g, 0)

    def frames(first, lanes):
        before = [g[first:4, :, lanes].reshape((4 - first) * COLS, 256)]
        if first:
            before.append(own_g[0:first, :, lanes].reshape(first * COLS, 256))
        return jnp.concatenate(before, axis=0)

    both = first_products(frames, 4, win_ref)
    bias = bin_ref[...].reshape(1, C)
    half_gain = 0.5 * gain_ref[...].reshape(1, C)
    not_first = jnp.where(lax.axis_index("tm") == 0, 0.0, 1.0)
    inside = edges(n)
    early = [not_first if keep is None else keep * not_first for keep in inside]
    for frame in range(4):
        activate(
            both, frame, bias, half_gain, early if frame < 2 else inside, feat.at[frame - 2] if frame >= 2 else None, d
        )

    bmid = bmid_ref[...].reshape(1, C)
    cells = [(k, e) for k in range(3) for e in range(3)]

    def weight(eta, a, k, e):
        lanes = slice(128 * k, 128 * (k + 1))
        if eta == 0:
            return w_ref[a, 0, e, :, lanes]
        if eta == 3:
            return w_ref[a, 2, e, :, lanes]
        return u_ref[eta - 1, a, e, :, lanes]

    def window(eta, a):
        rows = [d[eta, 128 * a : 512]]
        if a:
            rows.append(own_d[eta, 0 : 128 * a])
        return jnp.concatenate(rows, axis=0)

    def mix(tile):
        here = cells[2 * tile : 2 * tile + 2]
        m = []
        for eta in range(4):
            left = jnp.concatenate([window(eta, a) for a in range(3)], axis=1)
            right = jnp.concatenate(
                [jnp.concatenate([weight(eta, a, k, e) for k, e in here], axis=1) for a in range(3)], axis=0
            )
            m.append(jnp.dot(left, right, preferred_element_type=F32))
        total = ((m[1] + m[2]) + m[0], (m[1] - m[2]) - m[3])
        for place, (k, e) in enumerate(here):
            for y in range(2):
                mine = total[y][:, 128 * place : 128 * (place + 1)]
                for frame in range(4):
                    even = mine[128 * frame : 128 * frame + COLS]
                    odd = mine[128 * frame + COLS : 128 * (frame + 1)]
                    if e == 2:
                        up[y, k, frame, 0:COLS, :] = even
                    else:
                        part[y, 3 * k + e, 128 * frame : 128 * frame + COLS] = even
                    if e == 0:
                        down[y, k, frame, 8 : 8 + COLS, :] = odd
                    else:
                        part[y, 3 * k + e, 128 * frame + COLS : 128 * (frame + 1)] = odd

    def out_copy(k):
        at = (slice(None), slice(None), slice(None), slice(128 * k, 128 * (k + 1)))
        return pltpu.make_async_copy(made.at[at], out_ref.at[at], out_sem.at[k])

    def finish(k):
        ln = slice(128 * k, 128 * (k + 1))
        for frame in range(4):
            even_rows = slice(128 * frame, 128 * frame + COLS)
            odd_rows = slice(128 * frame + COLS, 128 * (frame + 1))
            have = feat.at[frame] if frame < 2 else own_feat.at[frame - 2]
            for y in range(2):
                even = down[y, k, frame, pl.ds(7, COLS), :] + part[y, 3 * k + 1, even_rows] + part[y, 3 * k + 2, odd_rows]
                odd = part[y, 3 * k, even_rows] + part[y, 3 * k + 1, odd_rows] + up[y, k, frame, pl.ds(1, COLS), :]
                even = have[y, 0, :, ln].astype(F32) + even + bmid[:, ln]
                odd = have[y, 1, :, ln].astype(F32) + odd + bmid[:, ln]
                slot = tmp.at[k, frame, y]
                slot[pl.ds(0, COLS, stride=2), :] = even
                slot[pl.ds(1, COLS, stride=2), :] = odd
                made[frame, y, :, ln] = slot[...].astype(BF16)
        out_copy(k).start()

    mix(0)
    mix(1)
    finish(0)
    mix(2)
    finish(1)
    mix(3)
    mix(4)
    finish(2)
    for k in range(3):
        out_copy(k).wait()


def block(r, win, pick, w, u, own_g, own_feat, own_d, b_in, gain, b_mid, tm_count, n):
    vm = pl.BlockSpec(memory_space=pltpu.VMEM)
    return pl.pallas_call(
        functools.partial(block_kernel, tm_count, n),
        out_shape=jax.ShapeDtypeStruct((4, 2, 2 * COLS, C), BF16),
        in_specs=[vm] * 11,
        out_specs=pl.BlockSpec(memory_space=pl.ANY),
        scratch_shapes=[
            pltpu.VMEM((6, 2 * COLS + 16, 128), F32),
            pltpu.VMEM((4, COLS, C), BF16),
            pltpu.VMEM((4, 4 * 128, C), BF16),
            pltpu.VMEM((2, 2, 2, COLS, C), BF16),
            pltpu.VMEM((2, 9, 512, 128), F32),
            pltpu.VMEM((2, 3, 4, COLS + 8, 128), F32),
            pltpu.VMEM((2, 3, 4, COLS + 8, 128), F32),
            pltpu.VMEM((3, 4, 2, 128, 128), F32),
            pltpu.VMEM((4, 2, 2 * COLS, C), BF16),
            pltpu.SemaphoreType.DMA((3,)),
        ],
        compiler_params=pltpu.CompilerParams(vmem_limit_bytes=28 << 20),
        name="block",
    )(r, win, pick, w, u, own_g, own_feat, own_d, b_in, gain, b_mid)


def solution(mesh):
    tm_count, n = mesh.shape["tm"], mesh.shape["space"]

    def per_device(tokens, w_in, b_in, gain, w_mid, b_mid):
        made = exchange(tokens[:, :, 0], w_in, w_mid, b_in, gain, tm_count, n)
        return block(*made, b_in, gain, b_mid, tm_count, n)

    return jax.shard_map(
        per_device,
        mesh=mesh,
        in_specs=(P("tm", None, "space", None), P(), P(), P(), P(), P()),
        out_specs=P("tm", "space", None, None),
        check_vma=False,
    )
```

time: 31.7 us -> 29.7 us (0.937)
  Pallas kernels: 31.6 us -> 29.6 us
    pallas_call x1, Pallas kernels: 11.5 us -> 10 us  [block(): pl.pallas_call(functools.partial(block_kernel, tm_count, n), out_shape=ja...]
    pallas_call x1, Pallas kernels: 20 us -> 19.6 us  [exchange(): pl.pallas_call(functools.partial(exchange_kernel, tm_count, n), out_shape...]
where the time goes in v3:
time: 29.7 us; the launch traced here: 29.6 us
  Pallas kernels  29.6 us (100%)
    pallas_call x1, Pallas kernels, exchange(): pl.pallas_call(functools.partial(exchange_kernel, tm_count, n), out_shape...  19.6 us
    pallas_call x1, Pallas kernels, block(): pl.pallas_call(functools.partial(block_kernel, tm_count, n), out_shape=ja...  10 us

profile of v3, /device:TPU:1, one launch (start us, length us, event | category | flops | bytes accessed | tf_op | source)
XLA Modules:
  0.0 29.6 jit_solution(17410279635854158710)
XLA Ops:
  0.0 0.0 copy-start.1
  0.0 0.0 copy-start
  0.0 0.0 copy-start.2
  0.0 19.6 %exchange.1 = (bf16[2,3,64,2,128]{4,3,2,1,0:T(2,128)(2,1)S(1)}, bf16[768,1536]{1,0:T(8,128)(2,1)S(1)}, bf16[384,768]{1,0:T(8,128)(2,1)S(1)}, bf16[3,3,3,384,384]...) custom-call(bf16[4,64,64]{2,1,0:T(8,128)(2,1)} %bitcast.1, ...), custom_call_target="tpu_custom_call" | custom-call | tf_op jit(solution)/shard_map/exchange/pallas_call | solution.py:215
  19.6 0.0 copy-done.1
  19.6 0.0 copy-done
  19.6 0.0 copy-done.2
  19.6 10.0 %block.1 = bf16[4,2,128,384]{3,2,1,0:T(8,128)(2,1)} custom-call(bf16[2,3,64,2,128]{4,3,2,1,0:T(2,128)(2,1)S(1)} %get-tuple-element.13.r_ref, bf16[768,1536]{1,0:T(8,128)(2,1)S(1)} %get-tuple-element.14.win_ref, bf16[384,768]{1,0:T(8,128)(2,1)S(1)} %get-tuple-element.15.pick_ref, bf16[3,3,3,384,384]{4,3,2,1,0:T(8,128)(2,1)S(1)} %get-tuple-element.16.w_ref, ...), custom_call_target="tpu_custom_call" | custom-call | tf_op jit(solution)/shard_map/block/pallas_call | solution.py:345
Async XLA Ops:
  0.0 19.6 %copy-start.1 = (f32[384]{0:T(512)S(1)}, f32[384]{0:T(512)}, u32[]{:S(2)}) copy-start(f32[384]{0:T(512)} %gain_ref.1) | copy-start | bytes 4612
  0.0 19.6 %copy-start = (f32[384]{0:T(512)S(1)}, f32[384]{0:T(512)}, u32[]{:S(2)}) copy-start(f32[384]{0:T(512)} %bin_ref.1) | copy-start | bytes 4612
  0.0 19.6 %copy-start.2 = (f32[384]{0:T(512)S(1)}, f32[384]{0:T(512)}, u32[]{:S(2)}) copy-start(f32[384]{0:T(512)} %bmid_ref.1) | copy-start | bytes 4612

commit v4 on v3

--- a/solution.py
+++ b/solution.py
@@ -68,13 +68,13 @@
                 if keeps[rho] is not None:
                     scale = scale * keeps[rho]
                 half = v * scale * half_gain
-                s.append(half + half * jnp.tanh(half))
+                s.append((half + half * jnp.tanh(half)).astype(BF16))
             start = 128 * sub + COLS * parity + 16 * block_row
             at = slice(start, start + 16)
-            d[0, at] = (s[0] - s[2]).astype(BF16)
-            d[1, at] = (s[1] + s[2]).astype(BF16)
-            d[2, at] = (s[2] - s[1]).astype(BF16)
-            d[3, at] = (s[1] - s[3]).astype(BF16)
+            d[0, at] = s[0] - s[2]
+            d[1, at] = s[1] + s[2]
+            d[2, at] = s[2] - s[1]
+            d[3, at] = s[1] - s[3]
 
 
 def edges(n):
@@ -84,7 +84,7 @@
 
 def exchange_kernel(
     tm_count, n, tok_hbm, w_in_hbm, w_hbm, bin_hbm, gain_hbm,
-    r_ref, win_ref, pick_ref, w_ref, u_ref, g_ref, feat_ref, d_ref,
+    r_ref, win_ref, pick_ref, w_ref, u_ref, v_ref, g_ref, feat_ref, d_ref,
     tok, x, w_in, bin_ref, gain_ref, spread,
     send_sem, recv_sem, send_next, recv_prev, own_sem, tok_sem, w_in_sem, bin_sem, gain_sem, w_sem,
 ):
@@ -119,6 +119,17 @@
                 pl.semaphore_signal(barrier, inc=1, device_id=(tm - 1, peer), device_id_type=MESH)
 
     signal(peers[:40])
+
+    win_ref[...] = jnp.zeros(win_ref.shape, BF16)
+
+    lane = lax.broadcasted_iota(jnp.int32, (C, C), 1)
+    have = lax.broadcasted_iota(jnp.int32, (C, C), 0)
+    y, col, c = lane // 64, (lane // 16) % 4, lane % 16
+    shift = jnp.where(me == 0, -1, jnp.where(me == n - 1, 1, 0))
+    want = (y // 2 + shift) * 128 + (y % 2) * 32 + ((col + 1) % 2) * 16 + c
+    for fp in range(2):
+        pick_ref[:, C * fp : C * (fp + 1)] = jnp.where(have == want + 64 * fp, 1.0, 0.0).astype(BF16)
+
     copies[0].wait()
     for h in range(2):
         x[:, h, :] = jnp.concatenate([tok[2 * h], tok[2 * h + 1]], axis=1)
@@ -150,7 +161,6 @@
             ).start()
 
     copies[1].wait()
-    win_ref[...] = jnp.zeros(win_ref.shape, BF16)
     for a in range(3):
         for b in range(3):
             block = w_in[a, b].reshape(3 * LAT, C)
@@ -160,25 +170,25 @@
                     lanes = slice((2 * row + parity) * C, (2 * row + parity + 1) * C)
                     win_ref[start : start + 3 * LAT, lanes] = block
 
-    lane = lax.broadcasted_iota(jnp.int32, (C, C), 1)
-    have = lax.broadcasted_iota(jnp.int32, (C, C), 0)
-    y, col, c = lane // 64, (lane // 16) % 4, lane % 16
-    shift = jnp.where(me == 0, -1, jnp.where(me == n - 1, 1, 0))
-    want = (y // 2 + shift) * 128 + (y % 2) * 32 + ((col + 1) % 2) * 16 + c
-    for fp in range(2):
-        pick_ref[:, C * fp : C * (fp + 1)] = jnp.where(have == want + 64 * fp, 1.0, 0.0).astype(BF16)
-
     copies[4].wait()
 
-    @pl.loop(0, 9)
+    @pl.loop(0, 18)
     def _(i):
-        a, e = i // 3, i % 3
-        for part in range(3):
-            rows = slice(128 * part, 128 * (part + 1))
-            outer = 0.5 * (w_ref[a, 0, e, rows].astype(F32) + w_ref[a, 2, e, rows].astype(F32))
-            inner = 0.5 * w_ref[a, 1, e, rows].astype(F32)
-            u_ref[0, a, e, rows] = (outer + inner).astype(BF16)
-            u_ref[1, a, e, rows] = (outer - inner).astype(BF16)
+        e, base = i // 6, (i % 6) * 64
+        for k in range(4):
+            rows = pl.ds(pl.multiple_of(base + 16 * k, 16), 16)
+            by_row = []
+            for a in range(3):
+                w0, w1, w2 = (w_ref[a, b, e, rows].astype(F32) for b in range(3))
+                outer = w0 + w2
+                by_row.append((w0, outer + w1, outer - w1, w2))
+            for eta in (1, 2):
+                u_ref[eta - 1, 0, e, rows] = by_row[0][eta].astype(BF16)
+                u_ref[eta - 1, 1, e, rows] = by_row[2][eta].astype(BF16)
+            for eta in range(4):
+                outer, inner = by_row[0][eta] + by_row[2][eta], by_row[1][eta]
+                v_ref[0, eta, e, rows] = (outer + inner).astype(BF16)
+                v_ref[1, eta, e, rows] = (outer - inner).astype(BF16)
 
     def await_all(half, count, sem):
         whole = r_ref.at[half, :, pl.ds(0, count)]
@@ -219,13 +229,14 @@
             jax.ShapeDtypeStruct((3 * 4 * 4 * LAT, 4 * C), BF16),
             jax.ShapeDtypeStruct((C, 2 * C), BF16),
             jax.ShapeDtypeStruct(w.shape, BF16),
-            jax.ShapeDtypeStruct((2, 3, 3, C, C), BF16),
+            jax.ShapeDtypeStruct((2, 2, 3, C, C), BF16),
+            jax.ShapeDtypeStruct((2, 4, 3, C, C), BF16),
             jax.ShapeDtypeStruct((4, COLS, C), BF16),
             jax.ShapeDtypeStruct((2, 2, 2, COLS, C), BF16),
             jax.ShapeDtypeStruct((4, 2 * 128, C), BF16),
         ),
         in_specs=[hbm] * 5,
-        out_specs=[vm] * 8,
+        out_specs=[vm] * 9,
         scratch_shapes=[
             pltpu.VMEM(tok.shape, BF16),
             pltpu.VMEM((n, 2, 128), BF16),
@@ -235,14 +246,14 @@
             pltpu.VMEM((6, 2 * COLS + 16, 128), F32),
         ]
         + [pltpu.SemaphoreType.DMA] * 10,
-        compiler_params=pltpu.CompilerParams(collective_id=0, has_side_effects=True, vmem_limit_bytes=24 << 20),
+        compiler_params=pltpu.CompilerParams(collective_id=0, has_side_effects=True, vmem_limit_bytes=8 << 20),
         name="exchange",
     )(*(pltpu.with_memory_space_constraint(v, pltpu.HBM) for v in (tok, w_in, w, b_in, gain)))
 
 
 def block_kernel(
-    tm_count, n, r_ref, win_ref, pick_ref, w_ref, u_ref, own_g, own_feat, own_d, bin_ref, gain_ref, bmid_ref,
-    out_ref, spread, g, d, feat, part, down, up, tmp, made, out_sem,
+    tm_count, n, r_ref, win_ref, pick_ref, w_ref, u_ref, v_ref, own_g, own_feat, own_d, bin_ref, gain_ref, bmid_ref,
+    out_ref, spread, g, d, dd, feat, part, down, up, tmp, made, out_sem,
 ):
     down[:, :, :, 0:8, :] = jnp.zeros(down.shape[:3] + (8, 128), F32)
     up[:, :, :, COLS : COLS + 8, :] = jnp.zeros(up.shape[:3] + (8, 128), F32)
@@ -268,36 +279,47 @@
     bmid = bmid_ref[...].reshape(1, C)
     cells = [(k, e) for k in range(3) for e in range(3)]
 
-    def weight(eta, a, k, e):
+    def weight(xi, eta, k, e):
         lanes = slice(128 * k, 128 * (k + 1))
-        if eta == 0:
-            return w_ref[a, 0, e, :, lanes]
-        if eta == 3:
-            return w_ref[a, 2, e, :, lanes]
-        return u_ref[eta - 1, a, e, :, lanes]
-
-    def window(eta, a):
-        rows = [d[eta, 128 * a : 512]]
-        if a:
-            rows.append(own_d[eta, 0 : 128 * a])
-        return jnp.concatenate(rows, axis=0)
+        if xi in (1, 2):
+            return v_ref[xi - 1, eta, e, :, lanes]
+        if eta in (1, 2):
+            return u_ref[eta - 1, xi // 3, e, :, lanes]
+        return w_ref[2 * (xi // 3), 2 * (eta // 3), e, :, lanes]
+
+    def plane(eta, frame):
+        if frame < 4:
+            return d[eta, 128 * frame : 128 * (frame + 1)]
+        return own_d[eta, 128 * (frame - 4) : 128 * (frame - 3)]
+
+    for eta in range(4):
+        for pair in range(2):
+            at = slice(128 * pair, 128 * (pair + 1))
+            f = [plane(eta, 2 * pair + i) for i in range(4)]
+            dd[0, eta, at] = f[0] - f[2]
+            dd[1, eta, at] = f[1] + f[2]
+            dd[2, eta, at] = f[2] - f[1]
+            dd[3, eta, at] = f[1] - f[3]
+
+    def combine(m):
+        return 0.5 * (m[1] + m[2]) + m[0], 0.5 * (m[1] - m[2]) - m[3]
 
     def mix(tile):
         here = cells[2 * tile : 2 * tile + 2]
-        m = []
-        for eta in range(4):
-            left = jnp.concatenate([window(eta, a) for a in range(3)], axis=1)
-            right = jnp.concatenate(
-                [jnp.concatenate([weight(eta, a, k, e) for k, e in here], axis=1) for a in range(3)], axis=0
-            )
-            m.append(jnp.dot(left, right, preferred_element_type=F32))
-        total = ((m[1] + m[2]) + m[0], (m[1] - m[2]) - m[3])
-        for place, (k, e) in enumerate(here):
-            for y in range(2):
-                mine = total[y][:, 128 * place : 128 * (place + 1)]
+        by_frame = []
+        for xi in range(4):
+            m = []
+            for eta in range(4):
+                right = jnp.concatenate([weight(xi, eta, k, e) for k, e in here], axis=1)
+                m.append(jnp.dot(dd[xi, eta], right, preferred_element_type=F32))
+            by_frame.append(combine(m))
+        for y in range(2):
+            total = combine([s[y] for s in by_frame])
+            for place, (k, e) in enumerate(here):
                 for frame in range(4):
-                    even = mine[128 * frame : 128 * frame + COLS]
-                    odd = mine[128 * frame + COLS : 128 * (frame + 1)]
+                    rows = 128 * (frame // 2)
+                    mine = total[frame % 2][rows : rows + 128, 128 * place : 128 * (place + 1)]
+                    even, odd = mine[:COLS], mine[COLS:]
                     if e == 2:
                         up[y, k, frame, 0:COLS, :] = even
                     else:
@@ -340,17 +362,18 @@
         out_copy(k).wait()
 
 
-def block(r, win, pick, w, u, own_g, own_feat, own_d, b_in, gain, b_mid, tm_count, n):
+def block(r, win, pick, w, u, v, own_g, own_feat, own_d, b_in, gain, b_mid, tm_count, n):
     vm = pl.BlockSpec(memory_space=pltpu.VMEM)
     return pl.pallas_call(
         functools.partial(block_kernel, tm_count, n),
         out_shape=jax.ShapeDtypeStruct((4, 2, 2 * COLS, C), BF16),
-        in_specs=[vm] * 11,
+        in_specs=[vm] * 12,
         out_specs=pl.BlockSpec(memory_space=pl.ANY),
         scratch_shapes=[
             pltpu.VMEM((6, 2 * COLS + 16, 128), F32),
             pltpu.VMEM((4, COLS, C), BF16),
             pltpu.VMEM((4, 4 * 128, C), BF16),
+            pltpu.VMEM((4, 4, 2 * 128, C), BF16),
             pltpu.VMEM((2, 2, 2, COLS, C), BF16),
             pltpu.VMEM((2, 9, 512, 128), F32),
             pltpu.VMEM((2, 3, 4, COLS + 8, 128), F32),
@@ -359,9 +382,9 @@
             pltpu.VMEM((4, 2, 2 * COLS, C), BF16),
             pltpu.SemaphoreType.DMA((3,)),
         ],
-        compiler_params=pltpu.CompilerParams(vmem_limit_bytes=28 << 20),
+        compiler_params=pltpu.CompilerParams(vmem_limit_bytes=22 << 20),
         name="block",
-    )(r, win, pick, w, u, own_g, own_feat, own_d, b_in, gain, b_mid)
+    )(r, win, pick, w, u, v, own_g, own_feat, own_d, b_in, gain, b_mid)
 
 
 def solution(mesh):

time: 29.7 us -> 29.3 us (0.987)
  Pallas kernels: 29.6 us -> 29.2 us
    pallas_call x1, Pallas kernels: 10 us -> 9.64 us  [block(): pl.pallas_call(functools.partial(block_kernel, tm_count, n), out_shape=ja...]
where the time goes in v4:
time: 29.3 us; the launch traced here: 29.2 us
  Pallas kernels  29.2 us (100%)
    pallas_call x1, Pallas kernels, exchange(): pl.pallas_call(functools.partial(exchange_kernel, tm_count, n), out_shape...  19.5 us
    pallas_call x1, Pallas kernels, block(): pl.pallas_call(functools.partial(block_kernel, tm_count, n), out_shape=ja...  9.64 us

profile of v4, /device:TPU:1, one launch (start us, length us, event | category | flops | bytes accessed | tf_op | source)
XLA Modules:
  0.0 29.2 jit_solution(2449323816487971941)
XLA Ops:
  0.0 0.0 copy-start.1
  0.0 0.0 copy-start
  0.0 0.0 copy-start.2
  0.0 19.5 %exchange.1 = (bf16[2,3,64,2,128]{4,3,2,1,0:T(2,128)(2,1)S(1)}, bf16[768,1536]{1,0:T(8,128)(2,1)S(1)}, bf16[384,768]{1,0:T(8,128)(2,1)S(1)}, bf16[3,3,3,384,384]...) custom-call(bf16[4,64,64]{2,1,0:T(8,128)(2,1)} %bitcast.1, ...), custom_call_target="tpu_custom_call" | custom-call | tf_op jit(solution)/shard_map/exchange/pallas_call | solution.py:225
  19.5 0.0 copy-done.1
  19.5 0.0 copy-done
  19.6 0.0 copy-done.2
  19.6 9.6 %block.1 = bf16[4,2,128,384]{3,2,1,0:T(8,128)(2,1)} custom-call(bf16[2,3,64,2,128]{4,3,2,1,0:T(2,128)(2,1)S(1)} %get-tuple-element.14.r_ref, bf16[768,1536]{1,0:T(8,128)(2,1)S(1)} %get-tuple-element.15.win_ref, bf16[384,768]{1,0:T(8,128)(2,1)S(1)} %get-tuple-element.16.pick_ref, bf16[3,3,3,384,384]{4,3,2,1,0:T(8,128)(2,1)S(1)} %get-tuple-element.17.w_ref, ...), custom_call_target="tpu_custom_call" | custom-call | tf_op jit(solution)/shard_map/block/pallas_call | solution.py:367
Async XLA Ops:
  0.0 19.5 %copy-start.1 = (f32[384]{0:T(512)S(1)}, f32[384]{0:T(512)}, u32[]{:S(2)}) copy-start(f32[384]{0:T(512)} %gain_ref.1) | copy-start | bytes 4612
  0.0 19.5 %copy-start = (f32[384]{0:T(512)S(1)}, f32[384]{0:T(512)}, u32[]{:S(2)}) copy-start(f32[384]{0:T(512)} %bin_ref.1) | copy-start | bytes 4612
  0.0 19.6 %copy-start.2 = (f32[384]{0:T(512)S(1)}, f32[384]{0:T(512)}, u32[]{:S(2)}) copy-start(f32[384]{0:T(512)} %bmid_ref.1) | copy-start | bytes 4612

commit v5 on v4

--- a/solution.py
+++ b/solution.py
@@ -329,9 +329,9 @@
                     else:
                         part[y, 3 * k + e, 128 * frame + COLS : 128 * (frame + 1)] = odd
 
-    def out_copy(k):
-        at = (slice(None), slice(None), slice(None), slice(128 * k, 128 * (k + 1)))
-        return pltpu.make_async_copy(made.at[at], out_ref.at[at], out_sem.at[k])
+    def out_copy(k, frame):
+        at = (frame, slice(None), slice(None), slice(128 * k, 128 * (k + 1)))
+        return pltpu.make_async_copy(made.at[at], out_ref.at[at], out_sem.at[k, frame])
 
     def finish(k):
         ln = slice(128 * k, 128 * (k + 1))
@@ -348,7 +348,7 @@
                 slot[pl.ds(0, COLS, stride=2), :] = even
                 slot[pl.ds(1, COLS, stride=2), :] = odd
                 made[frame, y, :, ln] = slot[...].astype(BF16)
-        out_copy(k).start()
+            out_copy(k, frame).start()
 
     mix(0)
     mix(1)
@@ -359,7 +359,8 @@
     mix(4)
     finish(2)
     for k in range(3):
-        out_copy(k).wait()
+        for frame in range(4):
+            out_copy(k, frame).wait()
 
 
 def block(r, win, pick, w, u, v, own_g, own_feat, own_d, b_in, gain, b_mid, tm_count, n):
@@ -380,7 +381,7 @@
             pltpu.VMEM((2, 3, 4, COLS + 8, 128), F32),
             pltpu.VMEM((3, 4, 2, 128, 128), F32),
             pltpu.VMEM((4, 2, 2 * COLS, C), BF16),
-            pltpu.SemaphoreType.DMA((3,)),
+            pltpu.SemaphoreType.DMA((3, 4)),
         ],
         compiler_params=pltpu.CompilerParams(vmem_limit_bytes=22 << 20),
         name="block",

time: 29.3 us -> 29.3 us (level)
  no operation moved by 1% of the time
where the time goes in v5:
time: 29.3 us; the launch traced here: 29.2 us
  Pallas kernels  29.1 us (99%)
    pallas_call x1, Pallas kernels, exchange(): pl.pallas_call(functools.partial(exchange_kernel, tm_count, n), out_shape...  19.5 us
    pallas_call x1, Pallas kernels, block(): pl.pallas_call(functools.partial(block_kernel, tm_count, n), out_shape=ja...  9.62 us

profile of v5, /device:TPU:1, one launch (start us, length us, event | category | flops | bytes accessed | tf_op | source)
XLA Modules:
  0.0 29.2 jit_solution(4347655085766956344)
XLA Ops:
  0.0 0.0 copy-start.1
  0.0 0.0 copy-start
  0.0 0.0 copy-start.2
  0.0 19.5 %exchange.1 = (bf16[2,3,64,2,128]{4,3,2,1,0:T(2,128)(2,1)S(1)}, bf16[768,1536]{1,0:T(8,128)(2,1)S(1)}, bf16[384,768]{1,0:T(8,128)(2,1)S(1)}, bf16[3,3,3,384,384]...) custom-call(bf16[4,64,64]{2,1,0:T(8,128)(2,1)} %bitcast.1, ...), custom_call_target="tpu_custom_call" | custom-call | tf_op jit(solution)/shard_map/exchange/pallas_call | solution.py:225
  19.5 0.0 copy-done.1
  19.5 0.0 copy-done
  19.6 0.0 copy-done.2
  19.6 9.6 %block.1 = bf16[4,2,128,384]{3,2,1,0:T(8,128)(2,1)} custom-call(bf16[2,3,64,2,128]{4,3,2,1,0:T(2,128)(2,1)S(1)} %get-tuple-element.14.r_ref, bf16[768,1536]{1,0:T(8,128)(2,1)S(1)} %get-tuple-element.15.win_ref, bf16[384,768]{1,0:T(8,128)(2,1)S(1)} %get-tuple-element.16.pick_ref, bf16[3,3,3,384,384]{4,3,2,1,0:T(8,128)(2,1)S(1)} %get-tuple-element.17.w_ref, ...), custom_call_target="tpu_custom_call" | custom-call | tf_op jit(solution)/shard_map/block/pallas_call | solution.py:368
Async XLA Ops:
  0.0 19.5 %copy-start.1 = (f32[384]{0:T(512)S(1)}, f32[384]{0:T(512)}, u32[]{:S(2)}) copy-start(f32[384]{0:T(512)} %gain_ref.1) | copy-start | bytes 4612
  0.0 19.5 %copy-start = (f32[384]{0:T(512)S(1)}, f32[384]{0:T(512)}, u32[]{:S(2)}) copy-start(f32[384]{0:T(512)} %bin_ref.1) | copy-start | bytes 4612
  0.0 19.6 %copy-start.2 = (f32[384]{0:T(512)S(1)}, f32[384]{0:T(512)}, u32[]{:S(2)}) copy-start(f32[384]{0:T(512)} %bmid_ref.1) | copy-start | bytes 4612
